TPU v7x, 32 devices: a whole 2x2x4 slice. The times are simulated.
32 devices in a mesh: ea: 16 (over z, y, x), ta: 2 (over core).
Axes of the slice: x: 2, y: 2, z: 4, core: 2. Of those that a mesh axis runs over, the one named last changes fastest.
Arguments:
- sample_inphase: float32 [128, 256, 256], P('ea'), may hold values from 0.2 to 1.2
- sample_quadrature: float32 [128, 256, 256], P('ea'), may hold values from -3 to 3
- beam_inphase: float32 [128, 3, 32, 32], P('ea'), may hold values from -3 to 3
- beam_quadrature: float32 [128, 3, 32, 32], P('ea'), may hold values from -3 to 3
- recorded_diffraction: float32 [128, 2, 16, 32, 32], P('ea', 'ta'), may hold values from 0.05 to 4
- window_corners: int32 [128, 2, 16, 2], P('ea', 'ta'), may hold values from 0 to 224
- filled_tallies: int32 [128, 2], P('ea', 'ta'), may hold values from 1 to 16, 24 in all within a row
- absorption_templates: float32 [16, 128], replicated, may hold values from -6 to 6
Outputs:
- fitted: float32 [2, 128, 16, 2, 2048], P(None, 'ea', None, 'ta')
- coefficients: float32 [2, 16, 65536], P(None, None, ('ea', 'ta'))
Inputs may be any that keep to these rules, and one draw needn't show every extreme that they name: `filled_tallies`: in each energy the two tiles' counts sum to 24 and the larger is at most 16. `window_corners`: offsets of slots at or past their tile's count are not used.
All inputs are finite; a program needn't handle non-finite values. No bound on the sum of `filled_tallies` on one device may be relied on, other than what follows from the above.
Results may differ from a plain program's by a relative error of at most 0.0003.
Values sent between devices are 32-bit elements; how exact they have to be, the bound alone decides.
No kernel may reach another device: no remote copies, remote signals or barrier semaphores. Data moves between devices by JAX's collectives and lax.ppermute only.
A program may use at most 64 MiB of HBM per device.

v0:
```python
import functools

import jax
import jax.numpy as jnp
import numpy as np
from jax import lax
from jax.experimental import pallas as pl
from jax.experimental.pallas import tpu as pltpu
from jax.sharding import Mesh
from jax.sharding import PartitionSpec as P

HIGHEST = lax.Precision.HIGHEST
FLOOR_POWER = 0.5
REGULARIZER = 1.0
LANES = 128
SUBS = 8
SMALL = 12 << 20
LARGE = 50 << 20


def split_bf16(x):
    hi = x.astype(jnp.bfloat16)
    lo = (x - hi.astype(jnp.float32)).astype(jnp.bfloat16)
    return hi, lo


def transform_tables(width):
    fold = LANES // width
    i = np.arange(LANES) // width
    k = np.arange(LANES) % width
    phase = np.outer(i, i) / fold + np.outer(k, k) / width
    m = np.exp(-2j * np.pi * phase) / width
    real = np.block([[m.real, m.imag], [-m.imag, m.real]])
    q = np.arange(SUBS)
    tw = np.exp(-2j * np.pi * np.outer(q, i) / width)
    tw = np.concatenate([tw.real, tw.imag]).astype(np.float32)

    def halves(a):
        hi = a.astype(jnp.bfloat16)
        lo = (a - hi.astype(np.float64)).astype(jnp.bfloat16)
        return np.concatenate([hi, hi, lo])

    return halves(real), halves(real.T.copy()), tw


def fft8(re, im, sign):
    def butterfly(a, b):
        return (a[0] + b[0], a[1] + b[1]), (a[0] - b[0], a[1] - b[1])

    def turn(a):
        return (-a[1], a[0]) if sign > 0 else (a[1], -a[0])

    h = np.float32(np.sqrt(0.5))

    def eighth(a):
        if sign > 0:
            return ((a[0] - a[1]) * h, (a[0] + a[1]) * h)
        return ((a[0] + a[1]) * h, (a[1] - a[0]) * h)

    def fft4(x):
        s0, d0 = butterfly(x[0], x[2])
        s1, d1 = butterfly(x[1], x[3])
        d1 = turn(d1)
        y0, y2 = butterfly(s0, s1)
        y1, y3 = butterfly(d0, d1)
        return [y0, y1, y2, y3]

    x = list(zip(re, im))
    e = fft4(x[0::2])
    o = fft4(x[1::2])
    o = [o[0], eighth(o[1]), turn(o[2]), turn(eighth(o[3]))]
    pairs = [butterfly(e[n], o[n]) for n in range(4)]
    out = [p[0] for p in pairs] + [p[1] for p in pairs]
    return [y[0] for y in out], [y[1] for y in out]


def step_kernel(
    n_e, spots, used, modes, width, dests, tiles,
    table_ref,
    o_re, o_im, pr_hbm, pi_hbm, own_rec, par_rec, wf_hbm, wb_hbm, tw_hbm,
    *refs,
):
    outs = refs[:dests], refs[dests:2 * dests]
    (
        obj, rec, beam, probe, wf_ref, wb_ref, tw_ref, patch, term, root, work,
        sum_re, sum_im, sum_light, stage, obj_sem, rec_sem, shared_sem, out_sem,
    ) = refs[2 * dests:]
    fold = LANES // width
    groups = used // SUBS
    per_group = modes * SUBS
    per_q = groups * per_group
    side = obj.shape[3]
    lead = table_ref[0] >> (2 * side.bit_length() - 2 + spots.bit_length())
    local = o_re.shape[0]
    first, me = lead & (local - 1), lead >> (local.bit_length() - 1)
    sums = (sum_re, sum_im, sum_light)

    def in_copies(e):
        return [
            pltpu.make_async_copy(
                ref.at[first + e, :, pl.ds(h * LANES, LANES)], obj.at[e, c, h], obj_sem.at[e, c, h]
            )
            for c, ref in enumerate((o_re, o_im))
            for h in range(2)
        ] + [
            pltpu.make_async_copy(own_rec.at[first + e], rec.at[e, pl.ds(0, spots)], rec_sem.at[e, 0]),
            pltpu.make_async_copy(par_rec.at[e], rec.at[e, pl.ds(spots, spots)], rec_sem.at[e, 1]),
        ]

    out_copies = [
        pltpu.make_async_copy(stage.at[c, d], outs[c][d], out_sem.at[c, d])
        for c in range(2)
        for d in range(dests)
    ]

    shared = [
        pltpu.make_async_copy(src, dst, shared_sem.at[n])
        for n, (src, dst) in enumerate(
            (
                (pr_hbm.at[pl.ds(first, n_e)], beam.at[0]),
                (pi_hbm.at[pl.ds(first, n_e)], beam.at[1]),
                (tw_hbm, tw_ref),
                (wf_hbm, wf_ref),
                (wb_hbm, wb_ref),
            )
        )
    ]
    for c in in_copies(0) + shared:
        c.start()
    lane = lax.broadcasted_iota(jnp.int32, (SUBS, LANES), 1)
    block = lane // width
    for c in shared:
        c.wait()

    def place(e, index):
        packed = table_ref[e * used + index]
        shift = side.bit_length() - 1
        return (packed >> (2 * shift)) & (2 * spots - 1), (packed >> shift) & (side - 1), packed & (side - 1)

    def merge(parts):
        out = parts[0]
        for n in range(1, fold):
            out = jnp.where(block == n, parts[n], out)
        return out

    def row_of(ref, *index):
        return jnp.broadcast_to(ref[index], (SUBS, LANES))

    def product(x, w_ref):
        hi, lo = split_bf16(x)
        wide = jnp.concatenate([hi, lo, hi], axis=1)
        return jnp.dot(wide, w_ref[...], preferred_element_type=jnp.float32)

    def energy(e, carry):
        for acc in sums:
            acc[...] = jnp.zeros_like(acc)
        for c in in_copies(e):
            c.wait()

        @pl.when(e + 1 < n_e)
        def _():
            for c in in_copies(e + 1):
                c.start()

        for c in range(2):
            for m in range(modes):
                probe[c, m] = jnp.concatenate(
                    [beam[c, e, m, pl.ds(i, SUBS, stride=fold), :] for i in range(fold)], axis=1
                )
        for s in range(used):
            slot, row, col = place(e, s)
            low = lane >= col
            for c in range(2):
                parts = []
                for i in range(fold):
                    at = pl.ds(row + i, SUBS, stride=fold)
                    v = jnp.where(low, obj[e, c, 0, at, :], obj[e, c, 1, at, :])
                    parts.append(pltpu.roll(v, (i * width - col) & (LANES - 1), 1))
                patch[c, s * SUBS:(s + 1) * SUBS, :] = merge(parts)
            root[s * SUBS:(s + 1) * SUBS, :] = jnp.concatenate(
                [rec[e, slot, r * SUBS:(r + 1) * SUBS, :] for r in range(fold)], axis=1
            )

        for g in range(groups):
            base = g * SUBS * SUBS
            ats = [pl.ds(base + t, SUBS, stride=SUBS) for t in range(SUBS)]
            w_re = [patch[0, at, :] for at in ats]
            w_im = [patch[1, at, :] for at in ats]
            for m in range(modes):
                x_re, x_im = [], []
                for t in range(SUBS):
                    p_re = row_of(probe, 0, m, pl.ds(t, 1), slice(None))
                    p_im = row_of(probe, 1, m, pl.ds(t, 1), slice(None))
                    x_re.append(p_re * w_re[t] - p_im * w_im[t])
                    x_im.append(p_re * w_im[t] + p_im * w_re[t])
                y_re, y_im = fft8(x_re, x_im, -1)
                for q in range(SUBS):
                    a, b = y_re[q], y_im[q]
                    if q:
                        c = row_of(tw_ref, pl.ds(q, 1), slice(None))
                        d = row_of(tw_ref, pl.ds(SUBS + q, 1), slice(None))
                        a, b = a * c - b * d, a * d + b * c
                    to = q * per_q + g * per_group + m * SUBS
                    work[to:to + SUBS, 0:LANES] = a
                    work[to:to + SUBS, LANES:2 * LANES] = b

        for part in range(2):
            qs = range(part * SUBS // 2, (part + 1) * SUBS // 2)
            rows = slice(qs[0] * per_q, (qs[-1] + 1) * per_q)
            z = product(work[rows, :], wf_ref)
            scaled = []
            for q in qs:
                for g in range(groups):
                    f = []
                    for m in range(modes):
                        at = (q - qs[0]) * per_q + g * per_group + m * SUBS
                        f.append((z[at:at + SUBS, 0:LANES], z[at:at + SUBS, LANES:2 * LANES]))
                    power = f[0][0] * f[0][0] + f[0][1] * f[0][1]
                    for a, b in f[1:]:
                        power = power + a * a + b * b
                    measured = root[pl.ds(g * SUBS * SUBS + q, SUBS, stride=SUBS), :]
                    factor = 1.0 - jnp.sqrt(measured) * lax.rsqrt(jnp.maximum(power, FLOOR_POWER))
                    scaled += [
                        jnp.concatenate([a * factor, b * factor], axis=1) for a, b in f
                    ]
            work[rows, :] = product(jnp.concatenate(scaled, axis=0), wb_ref)

        light = jnp.zeros((SUBS, LANES), jnp.float32)
        for m in range(modes):
            a, b = probe[0, m], probe[1, m]
            light = light + a * a + b * b

        for g in range(groups):
            t_re = [None] * SUBS
            t_im = [None] * SUBS
            for m in range(modes):
                x_re, x_im = [], []
                for q in range(SUBS):
                    frm = q * per_q + g * per_group + m * SUBS
                    a, b = work[frm:frm + SUBS, 0:LANES], work[frm:frm + SUBS, LANES:2 * LANES]
                    if q:
                        c = row_of(tw_ref, pl.ds(q, 1), slice(None))
                        d = row_of(tw_ref, pl.ds(SUBS + q, 1), slice(None))
                        a, b = a * c + b * d, b * c - a * d
                    x_re.append(a)
                    x_im.append(b)
                y_re, y_im = fft8(x_re, x_im, 1)
                for t in range(SUBS):
                    p_re = row_of(probe, 0, m, pl.ds(t, 1), slice(None))
                    p_im = row_of(probe, 1, m, pl.ds(t, 1), slice(None))
                    a = p_re * y_re[t] + p_im * y_im[t]
                    b = p_re * y_im[t] - p_im * y_re[t]
                    t_re[t] = a if m == 0 else t_re[t] + a
                    t_im[t] = b if m == 0 else t_im[t] + b
            for t in range(SUBS):
                at = pl.ds(g * SUBS * SUBS + t, SUBS, stride=SUBS)
                term[0, at, :] = t_re[t]
                term[1, at, :] = t_im[t]

        for s in range(used):
            _, row, col = place(e, s)
            frm = slice(s * SUBS, (s + 1) * SUBS)
            terms = (term[0, frm, :], term[1, frm, :], light)
            which = jnp.where(col <= LANES - width, 0, jnp.where(col >= LANES, 1, 2))
            start = jnp.where(col <= LANES - width, col, jnp.where(col >= LANES, col - LANES, col - LANES // 2))
            inside = (lane >= start) & (lane < start + width)
            ats = [pl.ds(row + i, SUBS, stride=fold) for i in range(fold)]
            for acc, t in zip(sums, terms):
                new = []
                for i in range(fold):
                    v = pltpu.roll(t, (start - i * width) & (LANES - 1), 1)
                    new.append(acc[which, ats[i], :] + jnp.where(inside, v, 0.0))
                for i in range(fold):
                    acc[which, ats[i], :] = new[i]

        high = lane >= LANES // 2

        def finish(k, carry):
            for u in range(SUBS):
                n = k * SUBS + u
                at = pl.ds(pl.multiple_of(n * SUBS, SUBS), SUBS)
                t, rest = n & (tiles - 1), n >> (tiles.bit_length() - 1)
                dest = (rest & (dests - 1)) ^ me
                to = (rest >> (dests.bit_length() - 1)) * tiles + t
                mid = [pltpu.roll(acc[2, at, :], LANES // 2, 1) for acc in sums]
                for h in range(2):
                    mine = high if h == 0 else ~high
                    full = [acc[h, at, :] + jnp.where(mine, m, 0.0) for acc, m in zip(sums, mid)]
                    share = 1.0 / (full[2] + REGULARIZER)
                    for c in range(2):
                        stage[c, dest, e, to, h] = obj[e, c, h, at, :] - full[c] * share
            return carry

        lax.fori_loop(0, side // SUBS // SUBS, finish, 0)
        return carry

    lax.fori_loop(0, n_e, energy, 0)
    for c in out_copies:
        c.start()
    for c in out_copies:
        c.wait()


def gradient_step(objects, beams, own_rec, par_rec, table, n_e, used, dests, tiles):
    o_re, o_im = objects
    _, side, _ = o_re.shape
    modes, width = beams[0].shape[1], beams[0].shape[-1]
    spots = own_rec.shape[1]
    flat = width * width // LANES
    assert flat == SUBS and side == 2 * LANES and used % SUBS == 0
    wf, wb, tw = transform_tables(width)
    hbm = pl.BlockSpec(memory_space=pl.ANY)
    out_shape = (n_e, side // SUBS // dests, side // LANES, SUBS, LANES)
    return pl.pallas_call(
        functools.partial(step_kernel, n_e, spots, used, modes, width, dests, tiles),
        out_shape=[jax.ShapeDtypeStruct(out_shape, jnp.float32)] * (2 * dests),
        grid_spec=pltpu.PrefetchScalarGridSpec(
            num_scalar_prefetch=1,
            grid=(1,),
            in_specs=[hbm] * 9,
            out_specs=[hbm] * (2 * dests),
            scratch_shapes=[
                pltpu.VMEM((n_e, 2, 2, side, LANES), jnp.float32),
                pltpu.VMEM((n_e, 2 * spots, width, width), jnp.float32),
                pltpu.VMEM((2, n_e, modes, width, width), jnp.float32),
                pltpu.VMEM((2, modes, flat, LANES), jnp.float32),
                *[pltpu.VMEM(wf.shape, jnp.bfloat16)] * 2,
                pltpu.VMEM(tw.shape, jnp.float32),
                pltpu.VMEM((2, used * SUBS, LANES), jnp.float32),
                pltpu.VMEM((2, used * SUBS, LANES), jnp.float32),
                pltpu.VMEM((used * SUBS, LANES), jnp.float32),
                pltpu.VMEM((SUBS * used * modes, 2 * LANES), jnp.float32),
                *[pltpu.VMEM((3, side, LANES), jnp.float32)] * 3,
                pltpu.VMEM((2, dests, *out_shape), jnp.float32),
                pltpu.SemaphoreType.DMA((n_e, 2, 2)),
                pltpu.SemaphoreType.DMA((n_e, 2)),
                pltpu.SemaphoreType.DMA((5,)),
                pltpu.SemaphoreType.DMA((2, dests)),
            ],
        ),
        compiler_params=pltpu.CompilerParams(vmem_limit_bytes=LARGE),
        name="gradient_step",
    )(
        table, o_re, o_im, *beams, own_rec, par_rec,
        jnp.asarray(wf), jnp.asarray(wb), jnp.asarray(tw),
    )


def slot_table(corners, theirs, counts, first, n_e, side, me):
    local, spots, _ = corners.shape
    lead = me * local + first
    assert local & (local - 1) == 0
    used = spots * 3 // 2
    assert side & (side - 1) == 0 and spots & (spots - 1) == 0
    both = jnp.concatenate([corners, theirs], axis=1)
    both = lax.dynamic_slice_in_dim(both, first, n_e, 0)
    counts = lax.dynamic_slice_in_dim(counts, first, n_e, 0)
    both = both[..., 0] * side + both[..., 1]
    both = both + (lead * 2 * spots + jnp.arange(2 * spots, dtype=jnp.int32)) * (side * side)
    index = jnp.arange(used, dtype=jnp.int32)[None]
    index = index + jnp.where(index < counts, 0, spots - counts)
    chosen = index[:, :, None] == jnp.arange(2 * spots, dtype=jnp.int32)
    return jnp.sum(jnp.where(chosen, both[:, None, :], 0), axis=2).reshape(-1)


def dot3(a, b):
    ah, al = split_bf16(a)
    bh, bl = split_bf16(b)
    left = jnp.concatenate([ah, al, ah], axis=1)
    right = jnp.concatenate([bh, bh, bl], axis=0)
    return jnp.dot(left, right, preferred_element_type=jnp.float32)


def solve_kernel(fars, cube, n_e, where_ref, basis_ref, project_ref, fit_ref):
    basis = basis_ref[...]
    edges, energies = basis.shape
    dot = functools.partial(lax.dot_general, precision=HIGHEST, preferred_element_type=jnp.float32)
    gram = dot(basis, basis, (((1,), (1,)), ((), ())))
    row = lax.broadcasted_iota(jnp.int32, (edges, 1), 0)
    right = basis
    for k in range(edges):
        pivot = 1.0 / gram[k:k + 1, k:k + 1]
        line, rhs = gram[k:k + 1, :] * pivot, right[k:k + 1, :] * pivot
        column = gram[:, k:k + 1]
        gram = jnp.where(row == k, line, gram - column * line)
        right = jnp.where(row == k, rhs, right - column * rhs)
    far, me, tile = where_ref[0], where_ref[1], where_ref[2]
    both = 2 * n_e

    def chosen(shape, axis, per, offset):
        n = lax.broadcasted_iota(jnp.int32, shape, axis)
        chip = (n // per) ^ me
        energy = far * (energies // fars) + chip * both + offset + n % per
        return (energy == lax.broadcasted_iota(jnp.int32, shape, 1 - axis)).astype(jnp.float32)

    project_ref[...] = dot(
        right, chosen((energies, cube * n_e), 1, n_e, tile * n_e), (((1,), (0,)), ((), ()))
    )
    fit_ref[...] = dot(
        chosen((cube * both, energies), 0, both, 0), basis, (((1,), (1,)), ((), ()))
    )


def solve_templates(where, basis, fars, cube, n_e):
    edges, _ = basis.shape
    vmem = pl.BlockSpec(memory_space=pltpu.VMEM)
    return pl.pallas_call(
        functools.partial(solve_kernel, fars, cube, n_e),
        out_shape=[
            jax.ShapeDtypeStruct((edges, cube * n_e), jnp.float32),
            jax.ShapeDtypeStruct((cube * 2 * n_e, edges), jnp.float32),
        ],
        in_specs=[pl.BlockSpec(memory_space=pltpu.SMEM), vmem],
        out_specs=[vmem] * 2,
        compiler_params=pltpu.CompilerParams(vmem_limit_bytes=SMALL),
        name="solve_templates",
    )(where, basis)


def project_kernel(fars, tiles, tile_ref, project_ref, *refs):
    *got, own_ref, other_ref, held = refs
    rows = got[0].shape[0]
    for d, ref in enumerate(got):
        held[d * rows:(d + 1) * rows, :] = ref[...]
    energies = project_ref.shape[1]
    stride = held.shape[0] // energies
    halves = stride // (fars * tiles * SUBS)
    for away, out_ref in enumerate((other_ref, own_ref)):
        tile = tile_ref[0] if away else 1 - tile_ref[0]
        for f in range(fars):
            for r in range(SUBS):
                parts = [
                    held[pl.ds(((f * tiles + tile) * halves + h) * SUBS + r, energies, stride=stride), :]
                    for h in range(halves)
                ]
                at = (f * SUBS + r) * halves * LANES
                values = jnp.concatenate(parts, axis=1)
                out_ref[:, at:at + halves * LANES] = dot3(project_ref[...], values)


def partial_coefs(tile, project, got, fars, tiles):
    rows = got[0].shape[0] * len(got)
    edges, energies = project.shape
    pixels = rows // energies // tiles * LANES
    vmem = pl.BlockSpec(memory_space=pltpu.VMEM)
    return pl.pallas_call(
        functools.partial(project_kernel, fars, tiles),
        out_shape=[jax.ShapeDtypeStruct((edges, pixels), jnp.float32)] * 2,
        in_specs=[pl.BlockSpec(memory_space=pltpu.SMEM)] + [vmem] * (1 + len(got)),
        out_specs=[vmem] * 2,
        scratch_shapes=[pltpu.VMEM((rows, LANES), jnp.float32)],
        cost_estimate=pl.CostEstimate(
            flops=6 * edges * energies * pixels, bytes_accessed=rows * LANES * 4, transcendentals=0
        ),
        compiler_params=pltpu.CompilerParams(vmem_limit_bytes=SMALL),
        name="partial_coefs",
    )(tile, project, *got)


def fit_kernel(far_ref, mine_ref, theirs_ref, basis_ref, coef_ref, *fit):
    own = coef_ref.shape[1]
    per = basis_ref.shape[0] // len(fit)
    stride = fit[0].shape[0] // per
    at = pl.ds(pl.multiple_of(far_ref[0] * own, own), own)
    coef_ref[...] = mine_ref[:, at] + theirs_ref[:, at]
    wide = 2 * LANES
    for j in range(mine_ref.shape[1] // wide):
        cols = slice(j * wide, (j + 1) * wide)
        values = dot3(basis_ref[...], mine_ref[:, cols] + theirs_ref[:, cols])
        for d, ref in enumerate(fit):
            for u in range(2):
                ref[pl.ds(j * 2 + u, per, stride=stride), :] = values[
                    d * per:(d + 1) * per, u * LANES:(u + 1) * LANES
                ]


def fitted_values(far, mine, theirs, basis, own, dests):
    edges, pixels = mine.shape
    energies = basis.shape[0]
    vmem = pl.BlockSpec(memory_space=pltpu.VMEM)
    rows = energies // dests * pixels // LANES
    out = pl.pallas_call(
        fit_kernel,
        out_shape=[jax.ShapeDtypeStruct((edges, own), jnp.float32)]
        + [jax.ShapeDtypeStruct((rows, LANES), jnp.float32)] * dests,
        in_specs=[pl.BlockSpec(memory_space=pltpu.SMEM), vmem, vmem, vmem],
        out_specs=[vmem] * (1 + dests),
        cost_estimate=pl.CostEstimate(
            flops=6 * edges * energies * pixels, bytes_accessed=energies * pixels * 4, transcendentals=0
        ),
        compiler_params=pltpu.CompilerParams(vmem_limit_bytes=SMALL),
        name="fitted_values",
    )(far, mine, theirs, basis)
    return out[0], out[1:]


def gather_kernel(part, senders, me_ref, *refs):
    got, (out_ref, sem) = refs[:senders], refs[-2:]
    copies = [
        pltpu.make_async_copy(ref, out_ref.at[part, :, :, me_ref[0] ^ d], sem.at[d])
        for d, ref in enumerate(got)
    ]
    for c in copies:
        c.start()
    for c in copies:
        c.wait()


def gather_part(part, me, got, out):
    senders = len(got)
    energies, fars, subs, _ = got[0].shape
    shape = (2, energies, fars, senders, subs, LANES)
    hbm = pl.BlockSpec(memory_space=pl.ANY)
    return pl.pallas_call(
        functools.partial(gather_kernel, part, senders),
        out_shape=jax.ShapeDtypeStruct(shape, jnp.float32),
        in_specs=[pl.BlockSpec(memory_space=pltpu.SMEM)]
        + [pl.BlockSpec(memory_space=pltpu.VMEM)] * senders
        + ([] if out is None else [hbm]),
        out_specs=hbm,
        scratch_shapes=[pltpu.SemaphoreType.DMA((senders,))],
        input_output_aliases={} if out is None else {1 + senders: 0},
        compiler_params=pltpu.CompilerParams(vmem_limit_bytes=SMALL),
        name="gather_part",
    )(me, *got, *([] if out is None else [out]))


def exchange(blocks, cube):
    return [
        b if d == 0 else lax.ppermute(b, "cube", [(i, i ^ d) for i in range(cube)])
        for d, b in enumerate(blocks)
    ]


def local(
    sample_inphase,
    sample_quadrature,
    beam_inphase,
    beam_quadrature,
    recorded_diffraction,
    window_corners,
    filled_tallies,
    absorption_templates,
):
    local_energies = sample_inphase.shape[0]
    side = sample_inphase.shape[1]
    spots = recorded_diffraction.shape[2]
    fars = lax.axis_size("far")
    cube = lax.axis_size("cube")
    blocks = fars * cube
    tiles = lax.axis_size("ta")
    tile = lax.axis_index("ta")
    swap = [(0, 1), (1, 0)]
    assert tiles == 2 and fars == 2
    used = spots * 3 // 2
    divided = local_energies % tiles == 0
    n_e = local_energies // tiles if divided else local_energies
    pix = side * side // (blocks * tiles)
    two_level = divided and pix == SUBS * side and local_energies == SUBS and cube & (cube - 1) == 0
    own_rec = recorded_diffraction[:, 0]
    first = tile * n_e if divided else jnp.zeros((), jnp.int32)
    theirs = lax.ppermute(window_corners, "ta", swap)
    give = lax.dynamic_slice_in_dim(own_rec, (1 - tile) * n_e, n_e, 0) if divided else own_rec
    par_rec = lax.ppermute(give, "ta", swap)
    table = slot_table(
        window_corners[:, 0], theirs[:, 0], filled_tallies, first.astype(jnp.int32), n_e, side,
        lax.axis_index("cube").astype(jnp.int32) if two_level else 0,
    )
    stepped = gradient_step(
        (sample_inphase, sample_quadrature),
        (beam_inphase, beam_quadrature),
        own_rec,
        par_rec,
        table,
        n_e,
        used,
        cube if two_level else 1,
        tiles,
    )

    if two_level:
        far = lax.axis_index("far").astype(jnp.int32)
        me = lax.axis_index("cube").astype(jnp.int32)
        where = jnp.stack([far, me, tile.astype(jnp.int32)])
        project_near, basis_near = solve_templates(where, absorption_templates, fars, cube, n_e)
        out, coefs = None, []
        parts = stepped[:cube], stepped[cube:]
        got = []
        for part in range(2):
            got.append(exchange(parts[part], cube))
        for part in range(2):
            blocks = [x.reshape(-1, LANES) for x in got[part]]
            kept, given = partial_coefs(
                tile.astype(jnp.int32)[None], project_near, blocks, fars, tiles
            )
            share = kept + lax.ppermute(given, "ta", swap)
            theirs = lax.ppermute(share, "far", swap)
            coef, fit = fitted_values(far[None], share, theirs, basis_near, pix, cube)
            coefs.append(coef)
            fit = [x.reshape(local_energies, fars, pix // LANES, LANES) for x in fit]
            back = exchange(fit, cube)
            out = gather_part(part, me[None], back, out)
        return (out.reshape(2, local_energies, cube * fars, 1, pix), jnp.stack(coefs))

    gram = jnp.dot(absorption_templates, absorption_templates.T, precision=HIGHEST)
    factor_low = jnp.linalg.cholesky(gram)
    project = jax.scipy.linalg.cho_solve((factor_low, True), absorption_templates)
    flat = jnp.stack([x.transpose(0, 1, 3, 2, 4) for x in stepped])
    if divided:
        flat = flat.reshape(2, n_e, blocks * tiles, pix)
        got = lax.all_to_all(flat, ("far", "cube", "ta"), 2, 1, tiled=True)
    else:
        flat = flat.reshape(2, n_e, blocks, tiles, pix)
        flat = lax.dynamic_index_in_dim(flat, tile, 3, keepdims=False)
        got = lax.all_to_all(flat, ("far", "cube"), 2, 1, tiled=True)
    values = got.reshape(2, -1, pix)
    coefs = jnp.einsum("ke,cen->ckn", project, values, precision=HIGHEST)
    fitted_here = jnp.einsum("ke,ckn->cen", absorption_templates, coefs, precision=HIGHEST)
    returned = lax.all_to_all(
        fitted_here[:, :, None, :], ("far", "cube"), split_axis=1, concat_axis=2, tiled=True
    )
    return (returned[:, :, :, None, :], coefs)


def solution(mesh):
    blocks, tiles = mesh.shape["ea"], mesh.shape["ta"]
    mesh = Mesh(mesh.devices.reshape(2, blocks // 2, tiles), ("far", "cube", "ta"))
    ea = ("far", "cube")
    in_specs = (
        P(ea, None, None),
        P(ea, None, None),
        P(ea, None, None, None),
        P(ea, None, None, None),
        P(ea, "ta", None, None, None),
        P(ea, "ta", None, None),
        P(ea, "ta"),
        P(),
    )
    out_specs = (P(None, ea, None, "ta", None), P(None, None, (*ea, "ta")))
    return jax.shard_map(local, mesh=mesh, in_specs=in_specs, out_specs=out_specs, check_vma=False)
```

profile of v0, /device:TPU:0, one launch (start us, length us, event | category | flops | bytes accessed | tf_op | source)
XLA Modules:
  0.0 110.8 jit_solution(4631395960098716596)
XLA Ops:
  1.3 2.3 %dynamic-slice_bitcast_fusion = f32[4,16,32,32]{3,2,1,0:T(8,128)} fusion(f32[8,1,16,32,32]{4,3,2,1,0:T(8,128)} %param.15, s32[]{:T(128)S(6)} %select_n.22), kind=kLoop, calls=%fused_computation | loop fusion | bytes 524292 | tf_op jit(solution)/shard_map/dynamic_slice | solution.py:563
  4.2 2.3 %collective-permute-done.1.par_rec = f32[4,16,32,32]{3,2,1,0:T(8,128)} collective-permute-done((f32[4,16,32,32]{3,2,1,0:T(8,128)}, f32[4,16,32,32]{3,2,1,0:T(8,128)}, u32[]{:S(2)}, u32[]{:S(2)}) %collective-permute-start.1) | collective-permute-done | bytes 262176 | tf_op jit(solution)/shard_map/ppermute | solution.py:564
  6.6 13.9 %gradient_step.1 = (f32[4,4,2,8,128]{4,3,2,1,0:T(8,128)S(1)}, f32[4,4,2,8,128]{4,3,2,1,0:T(8,128)S(1)}, f32[4,4,2,8,128]{4,3,2,1,0:T(8,128)S(1)}, f32[4,4,2,8,12...) custom-call(s32[96]{0:T(128)S(1)} %reshape.182.table_ref, ...), custom_call_target="tpu_custom_call" | custom-call | tf_op jit(solution)/shard_map/gradient_step/pallas_call | solution.py:314
  20.5 2.7 %collective-permute-start.2 = (f32[4,4,2,8,128]{4,3,2,1,0:T(8,128)S(1)}, f32[4,4,2,8,128]{4,3,2,1,0:T(8,128)S(1)}, u32[]{:S(2)}, u32[]{:S(2)}) collective-permute-start(f32[4,4,2,8,128]{4,3,2,1,0:T(8,128)S(1)} %get-tuple-element.44), channel_id=1, source_target_pairs={{0,2},{2,0},{4,6},{6,4},{8,10},{10,8},{12,14},{14,12},{1,3},{3,1},... | collective-permute-start | bytes 393224 | tf_op jit(solution)/shard_map/ppermute | solution.py:530
  23.1 1.5 %collective-permute-start.3 = (f32[4,4,2,8,128]{4,3,2,1,0:T(8,128)S(1)}, f32[4,4,2,8,128]{4,3,2,1,0:T(8,128)S(1)}, u32[]{:S(2)}, u32[]{:S(2)}) collective-permute-start(f32[4,4,2,8,128]{4,3,2,1,0:T(8,128)S(1)} %get-tuple-element.45), channel_id=1, source_target_pairs={{0,4},{2,6},{4,0},{6,2},{8,12},{10,14},{12,8},{14,10},{1,5},{3,7},... | collective-permute-start | bytes 393224 | tf_op jit(solution)/shard_map/ppermute | solution.py:530
  24.7 2.0 %collective-permute-start.5 = (f32[4,4,2,8,128]{4,3,2,1,0:T(8,128)S(1)}, f32[4,4,2,8,128]{4,3,2,1,0:T(8,128)S(1)}, u32[]{:S(2)}, u32[]{:S(2)}) collective-permute-start(f32[4,4,2,8,128]{4,3,2,1,0:T(8,128)S(1)} %get-tuple-element.47), channel_id=1, source_target_pairs={{0,8},{2,10},{4,12},{6,14},{8,0},{10,2},{12,4},{14,6},{1,9},{3,11}... | collective-permute-start | bytes 393224 | tf_op jit(solution)/shard_map/ppermute | solution.py:530
  26.7 1.4 %collective-permute-start.6 = (f32[4,4,2,8,128]{4,3,2,1,0:T(8,128)S(1)}, f32[4,4,2,8,128]{4,3,2,1,0:T(8,128)S(1)}, u32[]{:S(2)}, u32[]{:S(2)}) collective-permute-start(f32[4,4,2,8,128]{4,3,2,1,0:T(8,128)S(1)} %get-tuple-element.48), channel_id=1, source_target_pairs={{0,10},{2,8},{4,14},{6,12},{8,2},{10,0},{12,6},{14,4},{1,11},{3,9}... | collective-permute-start | bytes 393224 | tf_op jit(solution)/shard_map/ppermute | solution.py:530
  28.1 2.5 %collective-permute-start.7 = (f32[4,4,2,8,128]{4,3,2,1,0:T(8,128)S(1)}, f32[4,4,2,8,128]{4,3,2,1,0:T(8,128)S(1)}, u32[]{:S(2)}, u32[]{:S(2)}) collective-permute-start(f32[4,4,2,8,128]{4,3,2,1,0:T(8,128)S(1)} %get-tuple-element.49), channel_id=1, source_target_pairs={{0,12},{2,14},{4,8},{6,10},{8,4},{10,6},{12,0},{14,2},{1,13},{3,15... | collective-permute-start | bytes 393224 | tf_op jit(solution)/shard_map/ppermute | solution.py:530
  31.0 1.7 %collective-permute-start.8 = (f32[4,4,2,8,128]{4,3,2,1,0:T(8,128)S(1)}, f32[4,4,2,8,128]{4,3,2,1,0:T(8,128)S(1)}, u32[]{:S(2)}, u32[]{:S(2)}) collective-permute-start(f32[4,4,2,8,128]{4,3,2,1,0:T(8,128)S(1)} %get-tuple-element.50), channel_id=1, source_target_pairs={{0,14},{2,12},{4,10},{6,8},{8,6},{10,4},{12,2},{14,0},{1,15},{3,13... | collective-permute-start | bytes 393224 | tf_op jit(solution)/shard_map/ppermute | solution.py:530
  32.6 2.9 %collective-permute-start.18 = (f32[4,4,2,8,128]{4,3,2,1,0:T(8,128)S(1)}, f32[4,4,2,8,128]{4,3,2,1,0:T(8,128)S(1)}, u32[]{:S(2)}, u32[]{:S(2)}) collective-permute-start(f32[4,4,2,8,128]{4,3,2,1,0:T(8,128)S(1)} %get-tuple-element.63), channel_id=1, source_target_pairs={{0,2},{2,0},{4,6},{6,4},{8,10},{10,8},{12,14},{14,12},{1,3},{3,1},... | collective-permute-start | bytes 393224 | tf_op jit(solution)/shard_map/ppermute | solution.py:530
  35.5 1.5 %collective-permute-start.20 = (f32[4,4,2,8,128]{4,3,2,1,0:T(8,128)S(1)}, f32[4,4,2,8,128]{4,3,2,1,0:T(8,128)S(1)}, u32[]{:S(2)}, u32[]{:S(2)}) collective-permute-start(f32[4,4,2,8,128]{4,3,2,1,0:T(8,128)S(1)} %get-tuple-element.65), channel_id=1, source_target_pairs={{0,6},{2,4},{4,2},{6,0},{8,14},{10,12},{12,10},{14,8},{1,7},{3,5},... | collective-permute-start | bytes 393224 | tf_op jit(solution)/shard_map/ppermute | solution.py:530
  38.0 2.0 %collective-permute-start.21 = (f32[4,4,2,8,128]{4,3,2,1,0:T(8,128)S(1)}, f32[4,4,2,8,128]{4,3,2,1,0:T(8,128)S(1)}, u32[]{:S(2)}, u32[]{:S(2)}) collective-permute-start(f32[4,4,2,8,128]{4,3,2,1,0:T(8,128)S(1)} %get-tuple-element.66), channel_id=1, source_target_pairs={{0,8},{2,10},{4,12},{6,14},{8,0},{10,2},{12,4},{14,6},{1,9},{3,11}... | collective-permute-start | bytes 393224 | tf_op jit(solution)/shard_map/ppermute | solution.py:530
  39.9 1.9 %collective-permute-done.8 = f32[4,4,2,8,128]{4,3,2,1,0:T(8,128)S(1)} collective-permute-done((f32[4,4,2,8,128]{4,3,2,1,0:T(8,128)S(1)}, f32[4,4,2,8,128]{4,3,2,1,0:T(8,128)S(1)}, u32[]{:S(2)}, u32[]{:S(2)}) %collective-permute-start.8) | collective-permute-done | bytes 131104 | tf_op jit(solution)/shard_map/ppermute | solution.py:530
  41.8 1.6 %collective-permute-start.22 = (f32[4,4,2,8,128]{4,3,2,1,0:T(8,128)S(1)}, f32[4,4,2,8,128]{4,3,2,1,0:T(8,128)S(1)}, u32[]{:S(2)}, u32[]{:S(2)}) collective-permute-start(f32[4,4,2,8,128]{4,3,2,1,0:T(8,128)S(1)} %get-tuple-element.67), channel_id=1, source_target_pairs={{0,10},{2,8},{4,14},{6,12},{8,2},{10,0},{12,6},{14,4},{1,11},{3,9}... | collective-permute-start | bytes 393224 | tf_op jit(solution)/shard_map/ppermute | solution.py:530
  43.5 3.4 %collective-permute-done.19 = f32[4,4,2,8,128]{4,3,2,1,0:T(8,128)S(1)} collective-permute-done((f32[4,4,2,8,128]{4,3,2,1,0:T(8,128)S(1)}, f32[4,4,2,8,128]{4,3,2,1,0:T(8,128)S(1)}, u32[]{:S(2)}, u32[]{:S(2)}) %collective-permute-start.19) | collective-permute-done | bytes 131104 | tf_op jit(solution)/shard_map/ppermute | solution.py:530
  47.3 2.1 %solve_templates.1 = (f32[16,32]{1,0:T(8,128)S(1)}, f32[64,16]{1,0:T(8,128)S(1)}) custom-call(s32[3]{0:T(128)S(1)} %pad_add_fusion.where_ref, f32[16,128]{1,0:T(8,128)S(1)} %copy-done.4), custom_call_target="tpu_custom_call" | custom-call | tf_op jit(solution)/shard_map/solve_templates/pallas_call | solution.py:407
  50.3 3.3 %collective-permute-done.24 = f32[4,4,2,8,128]{4,3,2,1,0:T(8,128)S(1)} collective-permute-done((f32[4,4,2,8,128]{4,3,2,1,0:T(8,128)S(1)}, f32[4,4,2,8,128]{4,3,2,1,0:T(8,128)S(1)}, u32[]{:S(2)}, u32[]{:S(2)}) %collective-permute-start.24) | collective-permute-done | bytes 131104 | tf_op jit(solution)/shard_map/ppermute | solution.py:530
  54.4 2.9 %collective-permute-start.10 = (f32[16,4096]{1,0:T(8,128)S(1)}, f32[16,4096]{1,0:T(8,128)S(1)}, u32[]{:S(2)}, u32[]{:S(2)}) collective-permute-start(f32[16,4096]{1,0:T(8,128)S(1)} %add.74.mine_ref), channel_id=1, source_target_pairs={{0,16},{16,0},{1,17},{17,1},{2,18},{18,2},{3,19},{19,3},{4,20},{20... | collective-permute-start | bytes 786440 | tf_op jit(solution)/shard_map/ppermute | solution.py:597
  57.4 1.5 %collective-permute-start.26 = (f32[16,4096]{1,0:T(8,128)S(1)}, f32[16,4096]{1,0:T(8,128)S(1)}, u32[]{:S(2)}, u32[]{:S(2)}) collective-permute-start(f32[16,4096]{1,0:T(8,128)S(1)} %add.75.mine_ref), channel_id=1, source_target_pairs={{0,16},{16,0},{1,17},{17,1},{2,18},{18,2},{3,19},{19,3},{4,20},{20... | collective-permute-start | bytes 786440 | tf_op jit(solution)/shard_map/ppermute | solution.py:597
  58.8 17.0 %collective-permute-done.10.theirs_ref = f32[16,4096]{1,0:T(8,128)S(1)} collective-permute-done((f32[16,4096]{1,0:T(8,128)S(1)}, f32[16,4096]{1,0:T(8,128)S(1)}, u32[]{:S(2)}, u32[]{:S(2)}) %collective-permute-start.10) | collective-permute-done | bytes 262176 | tf_op jit(solution)/shard_map/ppermute | solution.py:597
  78.3 2.8 %collective-permute-done.26.theirs_ref = f32[16,4096]{1,0:T(8,128)S(1)} collective-permute-done((f32[16,4096]{1,0:T(8,128)S(1)}, f32[16,4096]{1,0:T(8,128)S(1)}, u32[]{:S(2)}, u32[]{:S(2)}) %collective-permute-start.26) | collective-permute-done | bytes 262176 | tf_op jit(solution)/shard_map/ppermute | solution.py:597
  83.5 2.0 %collective-permute-start.29 = (f32[8,2,16,128]{3,2,1,0:T(8,128)S(1)}, f32[8,2,16,128]{3,2,1,0:T(8,128)S(1)}, u32[]{:S(2)}, u32[]{:S(2)}) collective-permute-start(f32[8,2,16,128]{3,2,1,0:T(8,128)S(1)} %bitcast.78), channel_id=1, source_target_pairs={{0,6},{2,4},{4,2},{6,0},{8,14},{10,12},{12,10},{14,8},{1,7},{3,5},... | collective-permute-start | bytes 393224 | tf_op jit(solution)/shard_map/ppermute | solution.py:530
  86.0 1.9 %collective-permute-start.31 = (f32[8,2,16,128]{3,2,1,0:T(8,128)S(1)}, f32[8,2,16,128]{3,2,1,0:T(8,128)S(1)}, u32[]{:S(2)}, u32[]{:S(2)}) collective-permute-start(f32[8,2,16,128]{3,2,1,0:T(8,128)S(1)} %bitcast.75), channel_id=1, source_target_pairs={{0,10},{2,8},{4,14},{6,12},{8,2},{10,0},{12,6},{14,4},{1,11},{3,9}... | collective-permute-start | bytes 393224 | tf_op jit(solution)/shard_map/ppermute | solution.py:530
  88.4 1.9 %collective-permute-done.28.refs_2_ = f32[8,2,16,128]{3,2,1,0:T(8,128)S(1)} collective-permute-done((f32[8,2,16,128]{3,2,1,0:T(8,128)S(1)}, f32[8,2,16,128]{3,2,1,0:T(8,128)S(1)}, u32[]{:S(2)}, u32[]{:S(2)}) %collective-permute-start.28) | collective-permute-done | bytes 131104 | tf_op jit(solution)/shard_map/ppermute | solution.py:530
  91.4 1.7 %collective-permute-start.13 = (f32[8,2,16,128]{3,2,1,0:T(8,128)S(1)}, f32[8,2,16,128]{3,2,1,0:T(8,128)S(1)}, u32[]{:S(2)}, u32[]{:S(2)}) collective-permute-start(f32[8,2,16,128]{3,2,1,0:T(8,128)S(1)} %bitcast.72), channel_id=1, source_target_pairs={{0,6},{2,4},{4,2},{6,0},{8,14},{10,12},{12,10},{14,8},{1,7},{3,5},... | collective-permute-start | bytes 393224 | tf_op jit(solution)/shard_map/ppermute | solution.py:530
  93.1 1.6 %collective-permute-start.14 = (f32[8,2,16,128]{3,2,1,0:T(8,128)S(1)}, f32[8,2,16,128]{3,2,1,0:T(8,128)S(1)}, u32[]{:S(2)}, u32[]{:S(2)}) collective-permute-start(f32[8,2,16,128]{3,2,1,0:T(8,128)S(1)} %bitcast.71), channel_id=1, source_target_pairs={{0,8},{2,10},{4,12},{6,14},{8,0},{10,2},{12,4},{14,6},{1,9},{3,11}... | collective-permute-start | bytes 393224 | tf_op jit(solution)/shard_map/ppermute | solution.py:530
  96.2 1.4 %collective-permute-done.32.refs_6_ = f32[8,2,16,128]{3,2,1,0:T(8,128)S(1)} collective-permute-done((f32[8,2,16,128]{3,2,1,0:T(8,128)S(1)}, f32[8,2,16,128]{3,2,1,0:T(8,128)S(1)}, u32[]{:S(2)}, u32[]{:S(2)}) %collective-permute-start.32) | collective-permute-done | bytes 131104 | tf_op jit(solution)/shard_map/ppermute | solution.py:530
  97.6 1.9 %collective-permute-start.16 = (f32[8,2,16,128]{3,2,1,0:T(8,128)S(1)}, f32[8,2,16,128]{3,2,1,0:T(8,128)S(1)}, u32[]{:S(2)}, u32[]{:S(2)}) collective-permute-start(f32[8,2,16,128]{3,2,1,0:T(8,128)S(1)} %bitcast.69), channel_id=1, source_target_pairs={{0,12},{2,14},{4,8},{6,10},{8,4},{10,6},{12,0},{14,2},{1,13},{3,15... | collective-permute-start | bytes 393224 | tf_op jit(solution)/shard_map/ppermute | solution.py:530
  100.7 1.8 %collective-permute-start.17 = (f32[8,2,16,128]{3,2,1,0:T(8,128)S(1)}, f32[8,2,16,128]{3,2,1,0:T(8,128)S(1)}, u32[]{:S(2)}, u32[]{:S(2)}) collective-permute-start(f32[8,2,16,128]{3,2,1,0:T(8,128)S(1)} %bitcast.68), channel_id=1, source_target_pairs={{0,14},{2,12},{4,10},{6,8},{8,6},{10,4},{12,2},{14,0},{1,15},{3,13... | collective-permute-start | bytes 393224 | tf_op jit(solution)/shard_map/ppermute | solution.py:530
  104.3 2.0 %collective-permute-done.15.refs_5_ = f32[8,2,16,128]{3,2,1,0:T(8,128)S(1)} collective-permute-done((f32[8,2,16,128]{3,2,1,0:T(8,128)S(1)}, f32[8,2,16,128]{3,2,1,0:T(8,128)S(1)}, u32[]{:S(2)}, u32[]{:S(2)}) %collective-permute-start.15) | collective-permute-done | bytes 131104 | tf_op jit(solution)/shard_map/ppermute | solution.py:530
  106.3 1.6 %collective-permute-done.16.refs_6_ = f32[8,2,16,128]{3,2,1,0:T(8,128)S(1)} collective-permute-done((f32[8,2,16,128]{3,2,1,0:T(8,128)S(1)}, f32[8,2,16,128]{3,2,1,0:T(8,128)S(1)}, u32[]{:S(2)}, u32[]{:S(2)}) %collective-permute-start.16) | collective-permute-done | bytes 131104 | tf_op jit(solution)/shard_map/ppermute | solution.py:530
  107.9 1.9 %collective-permute-done.17.refs_7_ = f32[8,2,16,128]{3,2,1,0:T(8,128)S(1)} collective-permute-done((f32[8,2,16,128]{3,2,1,0:T(8,128)S(1)}, f32[8,2,16,128]{3,2,1,0:T(8,128)S(1)}, u32[]{:S(2)}, u32[]{:S(2)}) %collective-permute-start.17) | collective-permute-done | bytes 131104 | tf_op jit(solution)/shard_map/ppermute | solution.py:530
  (73 shorter events, 17.0 us)
Async XLA Ops:
  0.7 3.1 %collective-permute-start = (s32[8,1,16,2]{2,3,1,0:T(2,128)}, s32[8,1,16,2]{2,3,1,0:T(2,128)S(1)}, u32[]{:S(2)}, u32[]{:S(2)}) collective-permute-start(s32[8,1,16,2]{2,3,1,0:T(2,128)} %param.16), channel_id=1, source_target_pairs={{0,1},{1,0},{2,3},{3,2},{4,5},{5,4},{6,7},{7,6},{8,9},{9,8},{10,11... | collective-permute-start | bytes 3080 | tf_op jit(solution)/shard_map/ppermute | solution.py:562
  20.5 7.6 %collective-permute-start.2 = (f32[4,4,2,8,128]{4,3,2,1,0:T(8,128)S(1)}, f32[4,4,2,8,128]{4,3,2,1,0:T(8,128)S(1)}, u32[]{:S(2)}, u32[]{:S(2)}) collective-permute-start(f32[4,4,2,8,128]{4,3,2,1,0:T(8,128)S(1)} %get-tuple-element.44), channel_id=1, source_target_pairs={{0,2},{2,0},{4,6},{6,4},{8,10},{10,8},{12,14},{14,12},{1,3},{3,1},... | collective-permute-start | bytes 393224 | tf_op jit(solution)/shard_map/ppermute | solution.py:530
  23.1 7.8 %collective-permute-start.3 = (f32[4,4,2,8,128]{4,3,2,1,0:T(8,128)S(1)}, f32[4,4,2,8,128]{4,3,2,1,0:T(8,128)S(1)}, u32[]{:S(2)}, u32[]{:S(2)}) collective-permute-start(f32[4,4,2,8,128]{4,3,2,1,0:T(8,128)S(1)} %get-tuple-element.45), channel_id=1, source_target_pairs={{0,4},{2,6},{4,0},{6,2},{8,12},{10,14},{12,8},{14,10},{1,5},{3,7},... | collective-permute-start | bytes 393224 | tf_op jit(solution)/shard_map/ppermute | solution.py:530
  24.7 8.0 %collective-permute-start.4 = (f32[4,4,2,8,128]{4,3,2,1,0:T(8,128)S(1)}, f32[4,4,2,8,128]{4,3,2,1,0:T(8,128)S(1)}, u32[]{:S(2)}, u32[]{:S(2)}) collective-permute-start(f32[4,4,2,8,128]{4,3,2,1,0:T(8,128)S(1)} %get-tuple-element.46), channel_id=1, source_target_pairs={{0,6},{2,4},{4,2},{6,0},{8,14},{10,12},{12,10},{14,8},{1,7},{3,5},... | collective-permute-start | bytes 393224 | tf_op jit(solution)/shard_map/ppermute | solution.py:530
  24.7 10.8 %collective-permute-start.5 = (f32[4,4,2,8,128]{4,3,2,1,0:T(8,128)S(1)}, f32[4,4,2,8,128]{4,3,2,1,0:T(8,128)S(1)}, u32[]{:S(2)}, u32[]{:S(2)}) collective-permute-start(f32[4,4,2,8,128]{4,3,2,1,0:T(8,128)S(1)} %get-tuple-element.47), channel_id=1, source_target_pairs={{0,8},{2,10},{4,12},{6,14},{8,0},{10,2},{12,4},{14,6},{1,9},{3,11}... | collective-permute-start | bytes 393224 | tf_op jit(solution)/shard_map/ppermute | solution.py:530
  26.7 8.8 %collective-permute-start.6 = (f32[4,4,2,8,128]{4,3,2,1,0:T(8,128)S(1)}, f32[4,4,2,8,128]{4,3,2,1,0:T(8,128)S(1)}, u32[]{:S(2)}, u32[]{:S(2)}) collective-permute-start(f32[4,4,2,8,128]{4,3,2,1,0:T(8,128)S(1)} %get-tuple-element.48), channel_id=1, source_target_pairs={{0,10},{2,8},{4,14},{6,12},{8,2},{10,0},{12,6},{14,4},{1,11},{3,9}... | collective-permute-start | bytes 393224 | tf_op jit(solution)/shard_map/ppermute | solution.py:530
  28.1 9.8 %collective-permute-start.7 = (f32[4,4,2,8,128]{4,3,2,1,0:T(8,128)S(1)}, f32[4,4,2,8,128]{4,3,2,1,0:T(8,128)S(1)}, u32[]{:S(2)}, u32[]{:S(2)}) collective-permute-start(f32[4,4,2,8,128]{4,3,2,1,0:T(8,128)S(1)} %get-tuple-element.49), channel_id=1, source_target_pairs={{0,12},{2,14},{4,8},{6,10},{8,4},{10,6},{12,0},{14,2},{1,13},{3,15... | collective-permute-start | bytes 393224 | tf_op jit(solution)/shard_map/ppermute | solution.py:530
  31.0 10.8 %collective-permute-start.8 = (f32[4,4,2,8,128]{4,3,2,1,0:T(8,128)S(1)}, f32[4,4,2,8,128]{4,3,2,1,0:T(8,128)S(1)}, u32[]{:S(2)}, u32[]{:S(2)}) collective-permute-start(f32[4,4,2,8,128]{4,3,2,1,0:T(8,128)S(1)} %get-tuple-element.50), channel_id=1, source_target_pairs={{0,14},{2,12},{4,10},{6,8},{8,6},{10,4},{12,2},{14,0},{1,15},{3,13... | collective-permute-start | bytes 393224 | tf_op jit(solution)/shard_map/ppermute | solution.py:530
  32.6 10.7 %collective-permute-start.18 = (f32[4,4,2,8,128]{4,3,2,1,0:T(8,128)S(1)}, f32[4,4,2,8,128]{4,3,2,1,0:T(8,128)S(1)}, u32[]{:S(2)}, u32[]{:S(2)}) collective-permute-start(f32[4,4,2,8,128]{4,3,2,1,0:T(8,128)S(1)} %get-tuple-element.63), channel_id=1, source_target_pairs={{0,2},{2,0},{4,6},{6,4},{8,10},{10,8},{12,14},{14,12},{1,3},{3,1},... | collective-permute-start | bytes 393224 | tf_op jit(solution)/shard_map/ppermute | solution.py:530
  35.5 11.3 %collective-permute-start.19 = (f32[4,4,2,8,128]{4,3,2,1,0:T(8,128)S(1)}, f32[4,4,2,8,128]{4,3,2,1,0:T(8,128)S(1)}, u32[]{:S(2)}, u32[]{:S(2)}) collective-permute-start(f32[4,4,2,8,128]{4,3,2,1,0:T(8,128)S(1)} %get-tuple-element.64), channel_id=1, source_target_pairs={{0,4},{2,6},{4,0},{6,2},{8,12},{10,14},{12,8},{14,10},{1,5},{3,7},... | collective-permute-start | bytes 393224 | tf_op jit(solution)/shard_map/ppermute | solution.py:530
  35.5 14.7 %collective-permute-start.20 = (f32[4,4,2,8,128]{4,3,2,1,0:T(8,128)S(1)}, f32[4,4,2,8,128]{4,3,2,1,0:T(8,128)S(1)}, u32[]{:S(2)}, u32[]{:S(2)}) collective-permute-start(f32[4,4,2,8,128]{4,3,2,1,0:T(8,128)S(1)} %get-tuple-element.65), channel_id=1, source_target_pairs={{0,6},{2,4},{4,2},{6,0},{8,14},{10,12},{12,10},{14,8},{1,7},{3,5},... | collective-permute-start | bytes 393224 | tf_op jit(solution)/shard_map/ppermute | solution.py:530
  38.0 12.3 %collective-permute-start.21 = (f32[4,4,2,8,128]{4,3,2,1,0:T(8,128)S(1)}, f32[4,4,2,8,128]{4,3,2,1,0:T(8,128)S(1)}, u32[]{:S(2)}, u32[]{:S(2)}) collective-permute-start(f32[4,4,2,8,128]{4,3,2,1,0:T(8,128)S(1)} %get-tuple-element.66), channel_id=1, source_target_pairs={{0,8},{2,10},{4,12},{6,14},{8,0},{10,2},{12,4},{14,6},{1,9},{3,11}... | collective-permute-start | bytes 393224 | tf_op jit(solution)/shard_map/ppermute | solution.py:530
  41.8 8.5 %collective-permute-start.22 = (f32[4,4,2,8,128]{4,3,2,1,0:T(8,128)S(1)}, f32[4,4,2,8,128]{4,3,2,1,0:T(8,128)S(1)}, u32[]{:S(2)}, u32[]{:S(2)}) collective-permute-start(f32[4,4,2,8,128]{4,3,2,1,0:T(8,128)S(1)} %get-tuple-element.67), channel_id=1, source_target_pairs={{0,10},{2,8},{4,14},{6,12},{8,2},{10,0},{12,6},{14,4},{1,11},{3,9}... | collective-permute-start | bytes 393224 | tf_op jit(solution)/shard_map/ppermute | solution.py:530
  43.4 6.9 %collective-permute-start.23 = (f32[4,4,2,8,128]{4,3,2,1,0:T(8,128)S(1)}, f32[4,4,2,8,128]{4,3,2,1,0:T(8,128)S(1)}, u32[]{:S(2)}, u32[]{:S(2)}) collective-permute-start(f32[4,4,2,8,128]{4,3,2,1,0:T(8,128)S(1)} %get-tuple-element.68), channel_id=1, source_target_pairs={{0,12},{2,14},{4,8},{6,10},{8,4},{10,6},{12,0},{14,2},{1,13},{3,15... | collective-permute-start | bytes 393224 | tf_op jit(solution)/shard_map/ppermute | solution.py:530
  46.8 6.8 %collective-permute-start.24 = (f32[4,4,2,8,128]{4,3,2,1,0:T(8,128)S(1)}, f32[4,4,2,8,128]{4,3,2,1,0:T(8,128)S(1)}, u32[]{:S(2)}, u32[]{:S(2)}) collective-permute-start(f32[4,4,2,8,128]{4,3,2,1,0:T(8,128)S(1)} %get-tuple-element.69), channel_id=1, source_target_pairs={{0,14},{2,12},{4,10},{6,8},{8,6},{10,4},{12,2},{14,0},{1,15},{3,13... | collective-permute-start | bytes 393224 | tf_op jit(solution)/shard_map/ppermute | solution.py:530
  50.2 4.2 %collective-permute-start.9 = (f32[16,4096]{1,0:T(8,128)S(1)}, f32[16,4096]{1,0:T(8,128)S(1)}, u32[]{:S(2)}, u32[]{:S(2)}) collective-permute-start(f32[16,4096]{1,0:T(8,128)S(1)} %get-tuple-element.52), channel_id=1, source_target_pairs={{0,1},{1,0},{2,3},{3,2},{4,5},{5,4},{6,7},{7,6},{8,9},{9,8},{10,11... | collective-permute-start | bytes 786440 | tf_op jit(solution)/shard_map/ppermute | solution.py:596
  54.4 21.4 %collective-permute-start.10 = (f32[16,4096]{1,0:T(8,128)S(1)}, f32[16,4096]{1,0:T(8,128)S(1)}, u32[]{:S(2)}, u32[]{:S(2)}) collective-permute-start(f32[16,4096]{1,0:T(8,128)S(1)} %add.74.mine_ref), channel_id=1, source_target_pairs={{0,16},{16,0},{1,17},{17,1},{2,18},{18,2},{3,19},{19,3},{4,20},{20... | collective-permute-start | bytes 786440 | tf_op jit(solution)/shard_map/ppermute | solution.py:597
  57.4 23.8 %collective-permute-start.26 = (f32[16,4096]{1,0:T(8,128)S(1)}, f32[16,4096]{1,0:T(8,128)S(1)}, u32[]{:S(2)}, u32[]{:S(2)}) collective-permute-start(f32[16,4096]{1,0:T(8,128)S(1)} %add.75.mine_ref), channel_id=1, source_target_pairs={{0,16},{16,0},{1,17},{17,1},{2,18},{18,2},{3,19},{19,3},{4,20},{20... | collective-permute-start | bytes 786440 | tf_op jit(solution)/shard_map/ppermute | solution.py:597
  76.6 8.9 %collective-permute-start.11 = (f32[8,2,16,128]{3,2,1,0:T(8,128)S(1)}, f32[8,2,16,128]{3,2,1,0:T(8,128)S(1)}, u32[]{:S(2)}, u32[]{:S(2)}) collective-permute-start(f32[8,2,16,128]{3,2,1,0:T(8,128)S(1)} %bitcast.79), channel_id=1, source_target_pairs={{0,2},{2,0},{4,6},{6,4},{8,10},{10,8},{12,14},{14,12},{1,3},{3,1},... | collective-permute-start | bytes 393224 | tf_op jit(solution)/shard_map/ppermute | solution.py:530
  77.8 8.2 %collective-permute-start.12 = (f32[8,2,16,128]{3,2,1,0:T(8,128)S(1)}, f32[8,2,16,128]{3,2,1,0:T(8,128)S(1)}, u32[]{:S(2)}, u32[]{:S(2)}) collective-permute-start(f32[8,2,16,128]{3,2,1,0:T(8,128)S(1)} %bitcast.77), channel_id=1, source_target_pairs={{0,4},{2,6},{4,0},{6,2},{8,12},{10,14},{12,8},{14,10},{1,5},{3,7},... | collective-permute-start | bytes 393224 | tf_op jit(solution)/shard_map/ppermute | solution.py:530
  82.0 6.4 %collective-permute-start.27 = (f32[8,2,16,128]{3,2,1,0:T(8,128)S(1)}, f32[8,2,16,128]{3,2,1,0:T(8,128)S(1)}, u32[]{:S(2)}, u32[]{:S(2)}) collective-permute-start(f32[8,2,16,128]{3,2,1,0:T(8,128)S(1)} %bitcast.81), channel_id=1, source_target_pairs={{0,2},{2,0},{4,6},{6,4},{8,10},{10,8},{12,14},{14,12},{1,3},{3,1},... | collective-permute-start | bytes 393224 | tf_op jit(solution)/shard_map/ppermute | solution.py:530
  82.9 7.4 %collective-permute-start.28 = (f32[8,2,16,128]{3,2,1,0:T(8,128)S(1)}, f32[8,2,16,128]{3,2,1,0:T(8,128)S(1)}, u32[]{:S(2)}, u32[]{:S(2)}) collective-permute-start(f32[8,2,16,128]{3,2,1,0:T(8,128)S(1)} %bitcast.80), channel_id=1, source_target_pairs={{0,4},{2,6},{4,0},{6,2},{8,12},{10,14},{12,8},{14,10},{1,5},{3,7},... | collective-permute-start | bytes 393224 | tf_op jit(solution)/shard_map/ppermute | solution.py:530
  83.5 7.9 %collective-permute-start.29 = (f32[8,2,16,128]{3,2,1,0:T(8,128)S(1)}, f32[8,2,16,128]{3,2,1,0:T(8,128)S(1)}, u32[]{:S(2)}, u32[]{:S(2)}) collective-permute-start(f32[8,2,16,128]{3,2,1,0:T(8,128)S(1)} %bitcast.78), channel_id=1, source_target_pairs={{0,6},{2,4},{4,2},{6,0},{8,14},{10,12},{12,10},{14,8},{1,7},{3,5},... | collective-permute-start | bytes 393224 | tf_op jit(solution)/shard_map/ppermute | solution.py:530
  85.5 7.6 %collective-permute-start.30 = (f32[8,2,16,128]{3,2,1,0:T(8,128)S(1)}, f32[8,2,16,128]{3,2,1,0:T(8,128)S(1)}, u32[]{:S(2)}, u32[]{:S(2)}) collective-permute-start(f32[8,2,16,128]{3,2,1,0:T(8,128)S(1)} %bitcast.76), channel_id=1, source_target_pairs={{0,8},{2,10},{4,12},{6,14},{8,0},{10,2},{12,4},{14,6},{1,9},{3,11}... | collective-permute-start | bytes 393224 | tf_op jit(solution)/shard_map/ppermute | solution.py:530
  86.0 9.2 %collective-permute-start.31 = (f32[8,2,16,128]{3,2,1,0:T(8,128)S(1)}, f32[8,2,16,128]{3,2,1,0:T(8,128)S(1)}, u32[]{:S(2)}, u32[]{:S(2)}) collective-permute-start(f32[8,2,16,128]{3,2,1,0:T(8,128)S(1)} %bitcast.75), channel_id=1, source_target_pairs={{0,10},{2,8},{4,14},{6,12},{8,2},{10,0},{12,6},{14,4},{1,11},{3,9}... | collective-permute-start | bytes 393224 | tf_op jit(solution)/shard_map/ppermute | solution.py:530
  88.4 9.2 %collective-permute-start.32 = (f32[8,2,16,128]{3,2,1,0:T(8,128)S(1)}, f32[8,2,16,128]{3,2,1,0:T(8,128)S(1)}, u32[]{:S(2)}, u32[]{:S(2)}) collective-permute-start(f32[8,2,16,128]{3,2,1,0:T(8,128)S(1)} %bitcast.74), channel_id=1, source_target_pairs={{0,12},{2,14},{4,8},{6,10},{8,4},{10,6},{12,0},{14,2},{1,13},{3,15... | collective-permute-start | bytes 393224 | tf_op jit(solution)/shard_map/ppermute | solution.py:530
  90.3 10.4 %collective-permute-start.33 = (f32[8,2,16,128]{3,2,1,0:T(8,128)S(1)}, f32[8,2,16,128]{3,2,1,0:T(8,128)S(1)}, u32[]{:S(2)}, u32[]{:S(2)}) collective-permute-start(f32[8,2,16,128]{3,2,1,0:T(8,128)S(1)} %bitcast.73), channel_id=1, source_target_pairs={{0,14},{2,12},{4,10},{6,8},{8,6},{10,4},{12,2},{14,0},{1,15},{3,13... | collective-permute-start | bytes 393224 | tf_op jit(solution)/shard_map/ppermute | solution.py:530
  91.4 12.9 %collective-permute-start.13 = (f32[8,2,16,128]{3,2,1,0:T(8,128)S(1)}, f32[8,2,16,128]{3,2,1,0:T(8,128)S(1)}, u32[]{:S(2)}, u32[]{:S(2)}) collective-permute-start(f32[8,2,16,128]{3,2,1,0:T(8,128)S(1)} %bitcast.72), channel_id=1, source_target_pairs={{0,6},{2,4},{4,2},{6,0},{8,14},{10,12},{12,10},{14,8},{1,7},{3,5},... | collective-permute-start | bytes 393224 | tf_op jit(solution)/shard_map/ppermute | solution.py:530
  93.1 11.2 %collective-permute-start.14 = (f32[8,2,16,128]{3,2,1,0:T(8,128)S(1)}, f32[8,2,16,128]{3,2,1,0:T(8,128)S(1)}, u32[]{:S(2)}, u32[]{:S(2)}) collective-permute-start(f32[8,2,16,128]{3,2,1,0:T(8,128)S(1)} %bitcast.71), channel_id=1, source_target_pairs={{0,8},{2,10},{4,12},{6,14},{8,0},{10,2},{12,4},{14,6},{1,9},{3,11}... | collective-permute-start | bytes 393224 | tf_op jit(solution)/shard_map/ppermute | solution.py:530
  95.2 11.2 %collective-permute-start.15 = (f32[8,2,16,128]{3,2,1,0:T(8,128)S(1)}, f32[8,2,16,128]{3,2,1,0:T(8,128)S(1)}, u32[]{:S(2)}, u32[]{:S(2)}) collective-permute-start(f32[8,2,16,128]{3,2,1,0:T(8,128)S(1)} %bitcast.70), channel_id=1, source_target_pairs={{0,10},{2,8},{4,14},{6,12},{8,2},{10,0},{12,6},{14,4},{1,11},{3,9}... | collective-permute-start | bytes 393224 | tf_op jit(solution)/shard_map/ppermute | solution.py:530
  97.6 10.3 %collective-permute-start.16 = (f32[8,2,16,128]{3,2,1,0:T(8,128)S(1)}, f32[8,2,16,128]{3,2,1,0:T(8,128)S(1)}, u32[]{:S(2)}, u32[]{:S(2)}) collective-permute-start(f32[8,2,16,128]{3,2,1,0:T(8,128)S(1)} %bitcast.69), channel_id=1, source_target_pairs={{0,12},{2,14},{4,8},{6,10},{8,4},{10,6},{12,0},{14,2},{1,13},{3,15... | collective-permute-start | bytes 393224 | tf_op jit(solution)/shard_map/ppermute | solution.py:530
  100.7 9.1 %collective-permute-start.17 = (f32[8,2,16,128]{3,2,1,0:T(8,128)S(1)}, f32[8,2,16,128]{3,2,1,0:T(8,128)S(1)}, u32[]{:S(2)}, u32[]{:S(2)}) collective-permute-start(f32[8,2,16,128]{3,2,1,0:T(8,128)S(1)} %bitcast.68), channel_id=1, source_target_pairs={{0,14},{2,12},{4,10},{6,8},{8,6},{10,4},{12,2},{14,0},{1,15},{3,13... | collective-permute-start | bytes 393224 | tf_op jit(solution)/shard_map/ppermute | solution.py:530
  (10 other events, 82.2 us)
where the time goes:
time: 111 us
  waiting for transfers between devices  42.9 us (39%)
  starting transfers between devices  42.2 us (38%)
  Pallas kernels  21.2 us (19%)
  local copies, waits for them, and re-layouts  2.39 us (2%)
  other arithmetic  1.31 us (1%)
    ppermute x28, starting transfers between devices, exchange(): lax.ppermute(b, 'cube', [(i, i ^ d) for i in range(cube)])  37 us
    ppermute x28, waiting for transfers between devices, exchange(): lax.ppermute(b, 'cube', [(i, i ^ d) for i in range(cube)])  20.7 us
    ppermute x2, waiting for transfers between devices, local(): theirs = lax.ppermute(share, 'far', swap)  19.8 us
    pallas_call x1, Pallas kernels, gradient_step(): pl.pallas_call(functools.partial(step_kernel, n_e, spots, used, modes, wi...  13.9 us
    ppermute x2, starting transfers between devices, local(): theirs = lax.ppermute(share, 'far', swap)  4.36 us
    ppermute x1, waiting for transfers between devices, local(): par_rec = lax.ppermute(give, 'ta', swap)  2.3 us
    dynamic_slice x1, local copies, waits for them, and re-layouts, local(): lax.dynamic_slice_in_dim(own_rec, (1 - tile) * n_e, n_e, 0)  2.26 us
  transfers between devices with their start and end apart: 34, of which 16 were waited for; matrix products, arithmetic and copies ran while one was open for 3% of the time, Pallas kernels for 6%

commit v1 on v0

--- a/solution.py
+++ b/solution.py
@@ -83,7 +83,7 @@
     outs = refs[:dests], refs[dests:2 * dests]
     (
         obj, rec, beam, probe, wf_ref, wb_ref, tw_ref, patch, term, root, work,
-        sum_re, sum_im, sum_light, stage, obj_sem, rec_sem, shared_sem, out_sem,
+        sum_re, sum_im, sum_light, obj_sem, rec_sem, shared_sem,
     ) = refs[2 * dests:]
     fold = LANES // width
     groups = used // SUBS
@@ -106,12 +106,6 @@
             pltpu.make_async_copy(own_rec.at[first + e], rec.at[e, pl.ds(0, spots)], rec_sem.at[e, 0]),
             pltpu.make_async_copy(par_rec.at[e], rec.at[e, pl.ds(spots, spots)], rec_sem.at[e, 1]),
         ]
-
-    out_copies = [
-        pltpu.make_async_copy(stage.at[c, d], outs[c][d], out_sem.at[c, d])
-        for c in range(2)
-        for d in range(dests)
-    ]
 
     shared = [
         pltpu.make_async_copy(src, dst, shared_sem.at[n])
@@ -276,29 +270,22 @@
         high = lane >= LANES // 2
 
         def finish(k, carry):
-            for u in range(SUBS):
-                n = k * SUBS + u
+            for d in range(dests):
+                n = ((k >> (tiles.bit_length() - 1)) * dests + (d ^ me)) * tiles + (k & (tiles - 1))
                 at = pl.ds(pl.multiple_of(n * SUBS, SUBS), SUBS)
-                t, rest = n & (tiles - 1), n >> (tiles.bit_length() - 1)
-                dest = (rest & (dests - 1)) ^ me
-                to = (rest >> (dests.bit_length() - 1)) * tiles + t
                 mid = [pltpu.roll(acc[2, at, :], LANES // 2, 1) for acc in sums]
                 for h in range(2):
                     mine = high if h == 0 else ~high
                     full = [acc[h, at, :] + jnp.where(mine, m, 0.0) for acc, m in zip(sums, mid)]
                     share = 1.0 / (full[2] + REGULARIZER)
                     for c in range(2):
-                        stage[c, dest, e, to, h] = obj[e, c, h, at, :] - full[c] * share
+                        outs[c][d][e, k, h] = obj[e, c, h, at, :] - full[c] * share
             return carry
 
-        lax.fori_loop(0, side // SUBS // SUBS, finish, 0)
+        lax.fori_loop(0, side // SUBS // dests, finish, 0)
         return carry
 
     lax.fori_loop(0, n_e, energy, 0)
-    for c in out_copies:
-        c.start()
-    for c in out_copies:
-        c.wait()
 
 
 def gradient_step(objects, beams, own_rec, par_rec, table, n_e, used, dests, tiles):
@@ -318,7 +305,7 @@
             num_scalar_prefetch=1,
             grid=(1,),
             in_specs=[hbm] * 9,
-            out_specs=[hbm] * (2 * dests),
+            out_specs=[pl.BlockSpec(memory_space=pltpu.VMEM)] * (2 * dests),
             scratch_shapes=[
                 pltpu.VMEM((n_e, 2, 2, side, LANES), jnp.float32),
                 pltpu.VMEM((n_e, 2 * spots, width, width), jnp.float32),
@@ -331,11 +318,9 @@
                 pltpu.VMEM((used * SUBS, LANES), jnp.float32),
                 pltpu.VMEM((SUBS * used * modes, 2 * LANES), jnp.float32),
                 *[pltpu.VMEM((3, side, LANES), jnp.float32)] * 3,
-                pltpu.VMEM((2, dests, *out_shape), jnp.float32),
                 pltpu.SemaphoreType.DMA((n_e, 2, 2)),
                 pltpu.SemaphoreType.DMA((n_e, 2)),
                 pltpu.SemaphoreType.DMA((5,)),
-                pltpu.SemaphoreType.DMA((2, dests)),
             ],
         ),
         compiler_params=pltpu.CompilerParams(vmem_limit_bytes=LARGE),
@@ -526,10 +511,10 @@
 
 
 def exchange(blocks, cube):
-    return [
-        b if d == 0 else lax.ppermute(b, "cube", [(i, i ^ d) for i in range(cube)])
-        for d, b in enumerate(blocks)
-    ]
+    got = list(blocks)
+    for d in sorted(range(1, cube), key=lambda d: (-d.bit_count(), -d)):
+        got[d] = lax.ppermute(blocks[d], "cube", [(i, i ^ d) for i in range(cube)])
+    return got
 
 
 def local(

time: 111 us -> 108 us (0.973)
  Pallas kernels: 21.2 us -> 17.9 us
    pallas_call x1, Pallas kernels: 13.9 us -> 10.6 us  [gradient_step(): pl.pallas_call(functools.partial(step_kernel, n_e, spots, used, modes, wi...]
where the time goes in v1:
time: 108 us
  waiting for transfers between devices  43.2 us (40%)
  starting transfers between devices  42.1 us (39%)
  Pallas kernels  17.9 us (17%)
  local copies, waits for them, and re-layouts  2.39 us (2%)
  other arithmetic  1.31 us (1%)
    ppermute x28, starting transfers between devices, exchange(): got[d] = lax.ppermute(blocks[d], 'cube', [(i, i ^ d) for i in range(cube)])  36.9 us
    ppermute x28, waiting for transfers between devices, exchange(): got[d] = lax.ppermute(blocks[d], 'cube', [(i, i ^ d) for i in range(cube)])  21 us
    ppermute x2, waiting for transfers between devices, local(): theirs = lax.ppermute(share, 'far', swap)  19.8 us
    pallas_call x1, Pallas kernels, gradient_step(): pl.pallas_call(functools.partial(step_kernel, n_e, spots, used, modes, wi...  10.6 us
    ppermute x2, starting transfers between devices, local(): theirs = lax.ppermute(share, 'far', swap)  4.4 us
    ppermute x1, waiting for transfers between devices, local(): par_rec = lax.ppermute(give, 'ta', swap)  2.3 us
    dynamic_slice x1, local copies, waits for them, and re-layouts, local(): lax.dynamic_slice_in_dim(own_rec, (1 - tile) * n_e, n_e, 0)  2.26 us
  transfers between devices with their start and end apart: 34, of which 16 were waited for; matrix products, arithmetic and copies ran while one was open for 3% of the time, Pallas kernels for 6%

profile of v1, /device:TPU:0, one launch (start us, length us, event | category | flops | bytes accessed | tf_op | source)
XLA Modules:
  0.0 107.8 jit_solution(11159154414160327497)
XLA Ops:
  1.3 2.3 %dynamic-slice_bitcast_fusion = f32[4,16,32,32]{3,2,1,0:T(8,128)} fusion(f32[8,1,16,32,32]{4,3,2,1,0:T(8,128)} %param.15, s32[]{:T(128)S(6)} %select_n.22), kind=kLoop, calls=%fused_computation | loop fusion | bytes 524292 | tf_op jit(solution)/shard_map/dynamic_slice | solution.py:548
  4.2 2.3 %collective-permute-done.1.par_rec = f32[4,16,32,32]{3,2,1,0:T(8,128)} collective-permute-done((f32[4,16,32,32]{3,2,1,0:T(8,128)}, f32[4,16,32,32]{3,2,1,0:T(8,128)}, u32[]{:S(2)}, u32[]{:S(2)}) %collective-permute-start.1) | collective-permute-done | bytes 262176 | tf_op jit(solution)/shard_map/ppermute | solution.py:549
  6.6 10.6 %gradient_step.1 = (f32[4,4,2,8,128]{4,3,2,1,0:T(8,128)S(1)}, f32[4,4,2,8,128]{4,3,2,1,0:T(8,128)S(1)}, f32[4,4,2,8,128]{4,3,2,1,0:T(8,128)S(1)}, f32[4,4,2,8,12...) custom-call(s32[96]{0:T(128)S(1)} %reshape.182.table_ref, ...), custom_call_target="tpu_custom_call" | custom-call | tf_op jit(solution)/shard_map/gradient_step/pallas_call | solution.py:301
  17.2 2.7 %collective-permute-start.2 = (f32[4,4,2,8,128]{4,3,2,1,0:T(8,128)S(1)}, f32[4,4,2,8,128]{4,3,2,1,0:T(8,128)S(1)}, u32[]{:S(2)}, u32[]{:S(2)}) collective-permute-start(f32[4,4,2,8,128]{4,3,2,1,0:T(8,128)S(1)} %get-tuple-element.44), channel_id=1, source_target_pairs={{0,2},{2,0},{4,6},{6,4},{8,10},{10,8},{12,14},{14,12},{1,3},{3,1},... | collective-permute-start | bytes 393224 | tf_op jit(solution)/shard_map/ppermute | solution.py:516
  19.9 1.5 %collective-permute-start.3 = (f32[4,4,2,8,128]{4,3,2,1,0:T(8,128)S(1)}, f32[4,4,2,8,128]{4,3,2,1,0:T(8,128)S(1)}, u32[]{:S(2)}, u32[]{:S(2)}) collective-permute-start(f32[4,4,2,8,128]{4,3,2,1,0:T(8,128)S(1)} %get-tuple-element.45), channel_id=1, source_target_pairs={{0,4},{2,6},{4,0},{6,2},{8,12},{10,14},{12,8},{14,10},{1,5},{3,7},... | collective-permute-start | bytes 393224 | tf_op jit(solution)/shard_map/ppermute | solution.py:516
  21.4 2.0 %collective-permute-start.5 = (f32[4,4,2,8,128]{4,3,2,1,0:T(8,128)S(1)}, f32[4,4,2,8,128]{4,3,2,1,0:T(8,128)S(1)}, u32[]{:S(2)}, u32[]{:S(2)}) collective-permute-start(f32[4,4,2,8,128]{4,3,2,1,0:T(8,128)S(1)} %get-tuple-element.47), channel_id=1, source_target_pairs={{0,8},{2,10},{4,12},{6,14},{8,0},{10,2},{12,4},{14,6},{1,9},{3,11}... | collective-permute-start | bytes 393224 | tf_op jit(solution)/shard_map/ppermute | solution.py:516
  23.4 1.4 %collective-permute-start.6 = (f32[4,4,2,8,128]{4,3,2,1,0:T(8,128)S(1)}, f32[4,4,2,8,128]{4,3,2,1,0:T(8,128)S(1)}, u32[]{:S(2)}, u32[]{:S(2)}) collective-permute-start(f32[4,4,2,8,128]{4,3,2,1,0:T(8,128)S(1)} %get-tuple-element.48), channel_id=1, source_target_pairs={{0,10},{2,8},{4,14},{6,12},{8,2},{10,0},{12,6},{14,4},{1,11},{3,9}... | collective-permute-start | bytes 393224 | tf_op jit(solution)/shard_map/ppermute | solution.py:516
  24.8 2.5 %collective-permute-start.7 = (f32[4,4,2,8,128]{4,3,2,1,0:T(8,128)S(1)}, f32[4,4,2,8,128]{4,3,2,1,0:T(8,128)S(1)}, u32[]{:S(2)}, u32[]{:S(2)}) collective-permute-start(f32[4,4,2,8,128]{4,3,2,1,0:T(8,128)S(1)} %get-tuple-element.49), channel_id=1, source_target_pairs={{0,12},{2,14},{4,8},{6,10},{8,4},{10,6},{12,0},{14,2},{1,13},{3,15... | collective-permute-start | bytes 393224 | tf_op jit(solution)/shard_map/ppermute | solution.py:516
  27.7 1.7 %collective-permute-start.8 = (f32[4,4,2,8,128]{4,3,2,1,0:T(8,128)S(1)}, f32[4,4,2,8,128]{4,3,2,1,0:T(8,128)S(1)}, u32[]{:S(2)}, u32[]{:S(2)}) collective-permute-start(f32[4,4,2,8,128]{4,3,2,1,0:T(8,128)S(1)} %get-tuple-element.50), channel_id=1, source_target_pairs={{0,14},{2,12},{4,10},{6,8},{8,6},{10,4},{12,2},{14,0},{1,15},{3,13... | collective-permute-start | bytes 393224 | tf_op jit(solution)/shard_map/ppermute | solution.py:516
  29.4 2.9 %collective-permute-start.18 = (f32[4,4,2,8,128]{4,3,2,1,0:T(8,128)S(1)}, f32[4,4,2,8,128]{4,3,2,1,0:T(8,128)S(1)}, u32[]{:S(2)}, u32[]{:S(2)}) collective-permute-start(f32[4,4,2,8,128]{4,3,2,1,0:T(8,128)S(1)} %get-tuple-element.63), channel_id=1, source_target_pairs={{0,2},{2,0},{4,6},{6,4},{8,10},{10,8},{12,14},{14,12},{1,3},{3,1},... | collective-permute-start | bytes 393224 | tf_op jit(solution)/shard_map/ppermute | solution.py:516
  32.2 1.5 %collective-permute-start.20 = (f32[4,4,2,8,128]{4,3,2,1,0:T(8,128)S(1)}, f32[4,4,2,8,128]{4,3,2,1,0:T(8,128)S(1)}, u32[]{:S(2)}, u32[]{:S(2)}) collective-permute-start(f32[4,4,2,8,128]{4,3,2,1,0:T(8,128)S(1)} %get-tuple-element.65), channel_id=1, source_target_pairs={{0,6},{2,4},{4,2},{6,0},{8,14},{10,12},{12,10},{14,8},{1,7},{3,5},... | collective-permute-start | bytes 393224 | tf_op jit(solution)/shard_map/ppermute | solution.py:516
  34.7 1.9 %collective-permute-start.21 = (f32[4,4,2,8,128]{4,3,2,1,0:T(8,128)S(1)}, f32[4,4,2,8,128]{4,3,2,1,0:T(8,128)S(1)}, u32[]{:S(2)}, u32[]{:S(2)}) collective-permute-start(f32[4,4,2,8,128]{4,3,2,1,0:T(8,128)S(1)} %get-tuple-element.66), channel_id=1, source_target_pairs={{0,8},{2,10},{4,12},{6,14},{8,0},{10,2},{12,4},{14,6},{1,9},{3,11}... | collective-permute-start | bytes 393224 | tf_op jit(solution)/shard_map/ppermute | solution.py:516
  36.5 2.0 %collective-permute-done.8 = f32[4,4,2,8,128]{4,3,2,1,0:T(8,128)S(1)} collective-permute-done((f32[4,4,2,8,128]{4,3,2,1,0:T(8,128)S(1)}, f32[4,4,2,8,128]{4,3,2,1,0:T(8,128)S(1)}, u32[]{:S(2)}, u32[]{:S(2)}) %collective-permute-start.8) | collective-permute-done | bytes 131104 | tf_op jit(solution)/shard_map/ppermute | solution.py:516
  38.5 1.6 %collective-permute-start.22 = (f32[4,4,2,8,128]{4,3,2,1,0:T(8,128)S(1)}, f32[4,4,2,8,128]{4,3,2,1,0:T(8,128)S(1)}, u32[]{:S(2)}, u32[]{:S(2)}) collective-permute-start(f32[4,4,2,8,128]{4,3,2,1,0:T(8,128)S(1)} %get-tuple-element.67), channel_id=1, source_target_pairs={{0,10},{2,8},{4,14},{6,12},{8,2},{10,0},{12,6},{14,4},{1,11},{3,9}... | collective-permute-start | bytes 393224 | tf_op jit(solution)/shard_map/ppermute | solution.py:516
  40.2 3.4 %collective-permute-done.19 = f32[4,4,2,8,128]{4,3,2,1,0:T(8,128)S(1)} collective-permute-done((f32[4,4,2,8,128]{4,3,2,1,0:T(8,128)S(1)}, f32[4,4,2,8,128]{4,3,2,1,0:T(8,128)S(1)}, u32[]{:S(2)}, u32[]{:S(2)}) %collective-permute-start.19) | collective-permute-done | bytes 131104 | tf_op jit(solution)/shard_map/ppermute | solution.py:516
  44.0 2.1 %solve_templates.1 = (f32[16,32]{1,0:T(8,128)S(1)}, f32[64,16]{1,0:T(8,128)S(1)}) custom-call(s32[3]{0:T(128)S(1)} %pad_add_fusion.where_ref, f32[16,128]{1,0:T(8,128)S(1)} %copy-done.4), custom_call_target="tpu_custom_call" | custom-call | tf_op jit(solution)/shard_map/solve_templates/pallas_call | solution.py:392
  47.0 3.3 %collective-permute-done.24 = f32[4,4,2,8,128]{4,3,2,1,0:T(8,128)S(1)} collective-permute-done((f32[4,4,2,8,128]{4,3,2,1,0:T(8,128)S(1)}, f32[4,4,2,8,128]{4,3,2,1,0:T(8,128)S(1)}, u32[]{:S(2)}, u32[]{:S(2)}) %collective-permute-start.24) | collective-permute-done | bytes 131104 | tf_op jit(solution)/shard_map/ppermute | solution.py:516
  51.1 2.9 %collective-permute-start.10 = (f32[16,4096]{1,0:T(8,128)S(1)}, f32[16,4096]{1,0:T(8,128)S(1)}, u32[]{:S(2)}, u32[]{:S(2)}) collective-permute-start(f32[16,4096]{1,0:T(8,128)S(1)} %add.74.mine_ref), channel_id=1, source_target_pairs={{0,16},{16,0},{1,17},{17,1},{2,18},{18,2},{3,19},{19,3},{4,20},{20... | collective-permute-start | bytes 786440 | tf_op jit(solution)/shard_map/ppermute | solution.py:582
  54.1 1.5 %collective-permute-start.26 = (f32[16,4096]{1,0:T(8,128)S(1)}, f32[16,4096]{1,0:T(8,128)S(1)}, u32[]{:S(2)}, u32[]{:S(2)}) collective-permute-start(f32[16,4096]{1,0:T(8,128)S(1)} %add.75.mine_ref), channel_id=1, source_target_pairs={{0,16},{16,0},{1,17},{17,1},{2,18},{18,2},{3,19},{19,3},{4,20},{20... | collective-permute-start | bytes 786440 | tf_op jit(solution)/shard_map/ppermute | solution.py:582
  55.6 16.9 %collective-permute-done.10.theirs_ref = f32[16,4096]{1,0:T(8,128)S(1)} collective-permute-done((f32[16,4096]{1,0:T(8,128)S(1)}, f32[16,4096]{1,0:T(8,128)S(1)}, u32[]{:S(2)}, u32[]{:S(2)}) %collective-permute-start.10) | collective-permute-done | bytes 262176 | tf_op jit(solution)/shard_map/ppermute | solution.py:582
  75.0 2.9 %collective-permute-done.26.theirs_ref = f32[16,4096]{1,0:T(8,128)S(1)} collective-permute-done((f32[16,4096]{1,0:T(8,128)S(1)}, f32[16,4096]{1,0:T(8,128)S(1)}, u32[]{:S(2)}, u32[]{:S(2)}) %collective-permute-start.26) | collective-permute-done | bytes 262176 | tf_op jit(solution)/shard_map/ppermute | solution.py:582
  80.3 1.9 %collective-permute-start.29 = (f32[8,2,16,128]{3,2,1,0:T(8,128)S(1)}, f32[8,2,16,128]{3,2,1,0:T(8,128)S(1)}, u32[]{:S(2)}, u32[]{:S(2)}) collective-permute-start(f32[8,2,16,128]{3,2,1,0:T(8,128)S(1)} %bitcast.78), channel_id=1, source_target_pairs={{0,6},{2,4},{4,2},{6,0},{8,14},{10,12},{12,10},{14,8},{1,7},{3,5},... | collective-permute-start | bytes 393224 | tf_op jit(solution)/shard_map/ppermute | solution.py:516
  82.7 1.9 %collective-permute-start.31 = (f32[8,2,16,128]{3,2,1,0:T(8,128)S(1)}, f32[8,2,16,128]{3,2,1,0:T(8,128)S(1)}, u32[]{:S(2)}, u32[]{:S(2)}) collective-permute-start(f32[8,2,16,128]{3,2,1,0:T(8,128)S(1)} %bitcast.75), channel_id=1, source_target_pairs={{0,10},{2,8},{4,14},{6,12},{8,2},{10,0},{12,6},{14,4},{1,11},{3,9}... | collective-permute-start | bytes 393224 | tf_op jit(solution)/shard_map/ppermute | solution.py:516
  85.1 2.2 %collective-permute-done.28.refs_2_ = f32[8,2,16,128]{3,2,1,0:T(8,128)S(1)} collective-permute-done((f32[8,2,16,128]{3,2,1,0:T(8,128)S(1)}, f32[8,2,16,128]{3,2,1,0:T(8,128)S(1)}, u32[]{:S(2)}, u32[]{:S(2)}) %collective-permute-start.28) | collective-permute-done | bytes 131104 | tf_op jit(solution)/shard_map/ppermute | solution.py:516
  88.1 1.6 %collective-permute-start.13 = (f32[8,2,16,128]{3,2,1,0:T(8,128)S(1)}, f32[8,2,16,128]{3,2,1,0:T(8,128)S(1)}, u32[]{:S(2)}, u32[]{:S(2)}) collective-permute-start(f32[8,2,16,128]{3,2,1,0:T(8,128)S(1)} %bitcast.72), channel_id=1, source_target_pairs={{0,6},{2,4},{4,2},{6,0},{8,14},{10,12},{12,10},{14,8},{1,7},{3,5},... | collective-permute-start | bytes 393224 | tf_op jit(solution)/shard_map/ppermute | solution.py:516
  89.7 2.0 %collective-permute-start.14 = (f32[8,2,16,128]{3,2,1,0:T(8,128)S(1)}, f32[8,2,16,128]{3,2,1,0:T(8,128)S(1)}, u32[]{:S(2)}, u32[]{:S(2)}) collective-permute-start(f32[8,2,16,128]{3,2,1,0:T(8,128)S(1)} %bitcast.71), channel_id=1, source_target_pairs={{0,8},{2,10},{4,12},{6,14},{8,0},{10,2},{12,4},{14,6},{1,9},{3,11}... | collective-permute-start | bytes 393224 | tf_op jit(solution)/shard_map/ppermute | solution.py:516
  93.0 1.3 %collective-permute-done.32.refs_6_ = f32[8,2,16,128]{3,2,1,0:T(8,128)S(1)} collective-permute-done((f32[8,2,16,128]{3,2,1,0:T(8,128)S(1)}, f32[8,2,16,128]{3,2,1,0:T(8,128)S(1)}, u32[]{:S(2)}, u32[]{:S(2)}) %collective-permute-start.32) | collective-permute-done | bytes 131104 | tf_op jit(solution)/shard_map/ppermute | solution.py:516
  94.3 2.0 %collective-permute-start.16 = (f32[8,2,16,128]{3,2,1,0:T(8,128)S(1)}, f32[8,2,16,128]{3,2,1,0:T(8,128)S(1)}, u32[]{:S(2)}, u32[]{:S(2)}) collective-permute-start(f32[8,2,16,128]{3,2,1,0:T(8,128)S(1)} %bitcast.69), channel_id=1, source_target_pairs={{0,12},{2,14},{4,8},{6,10},{8,4},{10,6},{12,0},{14,2},{1,13},{3,15... | collective-permute-start | bytes 393224 | tf_op jit(solution)/shard_map/ppermute | solution.py:516
  97.5 1.7 %collective-permute-start.17 = (f32[8,2,16,128]{3,2,1,0:T(8,128)S(1)}, f32[8,2,16,128]{3,2,1,0:T(8,128)S(1)}, u32[]{:S(2)}, u32[]{:S(2)}) collective-permute-start(f32[8,2,16,128]{3,2,1,0:T(8,128)S(1)} %bitcast.68), channel_id=1, source_target_pairs={{0,14},{2,12},{4,10},{6,8},{8,6},{10,4},{12,2},{14,0},{1,15},{3,13... | collective-permute-start | bytes 393224 | tf_op jit(solution)/shard_map/ppermute | solution.py:516
  101.0 2.0 %collective-permute-done.15.refs_5_ = f32[8,2,16,128]{3,2,1,0:T(8,128)S(1)} collective-permute-done((f32[8,2,16,128]{3,2,1,0:T(8,128)S(1)}, f32[8,2,16,128]{3,2,1,0:T(8,128)S(1)}, u32[]{:S(2)}, u32[]{:S(2)}) %collective-permute-start.15) | collective-permute-done | bytes 131104 | tf_op jit(solution)/shard_map/ppermute | solution.py:516
  103.0 1.8 %collective-permute-done.16.refs_6_ = f32[8,2,16,128]{3,2,1,0:T(8,128)S(1)} collective-permute-done((f32[8,2,16,128]{3,2,1,0:T(8,128)S(1)}, f32[8,2,16,128]{3,2,1,0:T(8,128)S(1)}, u32[]{:S(2)}, u32[]{:S(2)}) %collective-permute-start.16) | collective-permute-done | bytes 131104 | tf_op jit(solution)/shard_map/ppermute | solution.py:516
  104.8 2.0 %collective-permute-done.17.refs_7_ = f32[8,2,16,128]{3,2,1,0:T(8,128)S(1)} collective-permute-done((f32[8,2,16,128]{3,2,1,0:T(8,128)S(1)}, f32[8,2,16,128]{3,2,1,0:T(8,128)S(1)}, u32[]{:S(2)}, u32[]{:S(2)}) %collective-permute-start.17) | collective-permute-done | bytes 131104 | tf_op jit(solution)/shard_map/ppermute | solution.py:516
  (73 shorter events, 16.6 us)
Async XLA Ops:
  0.7 3.1 %collective-permute-start = (s32[8,1,16,2]{2,3,1,0:T(2,128)}, s32[8,1,16,2]{2,3,1,0:T(2,128)S(1)}, u32[]{:S(2)}, u32[]{:S(2)}) collective-permute-start(s32[8,1,16,2]{2,3,1,0:T(2,128)} %param.16), channel_id=1, source_target_pairs={{0,1},{1,0},{2,3},{3,2},{4,5},{5,4},{6,7},{7,6},{8,9},{9,8},{10,11... | collective-permute-start | bytes 3080 | tf_op jit(solution)/shard_map/ppermute | solution.py:547
  17.2 7.6 %collective-permute-start.2 = (f32[4,4,2,8,128]{4,3,2,1,0:T(8,128)S(1)}, f32[4,4,2,8,128]{4,3,2,1,0:T(8,128)S(1)}, u32[]{:S(2)}, u32[]{:S(2)}) collective-permute-start(f32[4,4,2,8,128]{4,3,2,1,0:T(8,128)S(1)} %get-tuple-element.44), channel_id=1, source_target_pairs={{0,2},{2,0},{4,6},{6,4},{8,10},{10,8},{12,14},{14,12},{1,3},{3,1},... | collective-permute-start | bytes 393224 | tf_op jit(solution)/shard_map/ppermute | solution.py:516
  19.9 7.8 %collective-permute-start.3 = (f32[4,4,2,8,128]{4,3,2,1,0:T(8,128)S(1)}, f32[4,4,2,8,128]{4,3,2,1,0:T(8,128)S(1)}, u32[]{:S(2)}, u32[]{:S(2)}) collective-permute-start(f32[4,4,2,8,128]{4,3,2,1,0:T(8,128)S(1)} %get-tuple-element.45), channel_id=1, source_target_pairs={{0,4},{2,6},{4,0},{6,2},{8,12},{10,14},{12,8},{14,10},{1,5},{3,7},... | collective-permute-start | bytes 393224 | tf_op jit(solution)/shard_map/ppermute | solution.py:516
  21.4 8.0 %collective-permute-start.4 = (f32[4,4,2,8,128]{4,3,2,1,0:T(8,128)S(1)}, f32[4,4,2,8,128]{4,3,2,1,0:T(8,128)S(1)}, u32[]{:S(2)}, u32[]{:S(2)}) collective-permute-start(f32[4,4,2,8,128]{4,3,2,1,0:T(8,128)S(1)} %get-tuple-element.46), channel_id=1, source_target_pairs={{0,6},{2,4},{4,2},{6,0},{8,14},{10,12},{12,10},{14,8},{1,7},{3,5},... | collective-permute-start | bytes 393224 | tf_op jit(solution)/shard_map/ppermute | solution.py:516
  21.4 10.8 %collective-permute-start.5 = (f32[4,4,2,8,128]{4,3,2,1,0:T(8,128)S(1)}, f32[4,4,2,8,128]{4,3,2,1,0:T(8,128)S(1)}, u32[]{:S(2)}, u32[]{:S(2)}) collective-permute-start(f32[4,4,2,8,128]{4,3,2,1,0:T(8,128)S(1)} %get-tuple-element.47), channel_id=1, source_target_pairs={{0,8},{2,10},{4,12},{6,14},{8,0},{10,2},{12,4},{14,6},{1,9},{3,11}... | collective-permute-start | bytes 393224 | tf_op jit(solution)/shard_map/ppermute | solution.py:516
  23.4 8.8 %collective-permute-start.6 = (f32[4,4,2,8,128]{4,3,2,1,0:T(8,128)S(1)}, f32[4,4,2,8,128]{4,3,2,1,0:T(8,128)S(1)}, u32[]{:S(2)}, u32[]{:S(2)}) collective-permute-start(f32[4,4,2,8,128]{4,3,2,1,0:T(8,128)S(1)} %get-tuple-element.48), channel_id=1, source_target_pairs={{0,10},{2,8},{4,14},{6,12},{8,2},{10,0},{12,6},{14,4},{1,11},{3,9}... | collective-permute-start | bytes 393224 | tf_op jit(solution)/shard_map/ppermute | solution.py:516
  24.8 9.8 %collective-permute-start.7 = (f32[4,4,2,8,128]{4,3,2,1,0:T(8,128)S(1)}, f32[4,4,2,8,128]{4,3,2,1,0:T(8,128)S(1)}, u32[]{:S(2)}, u32[]{:S(2)}) collective-permute-start(f32[4,4,2,8,128]{4,3,2,1,0:T(8,128)S(1)} %get-tuple-element.49), channel_id=1, source_target_pairs={{0,12},{2,14},{4,8},{6,10},{8,4},{10,6},{12,0},{14,2},{1,13},{3,15... | collective-permute-start | bytes 393224 | tf_op jit(solution)/shard_map/ppermute | solution.py:516
  27.7 10.8 %collective-permute-start.8 = (f32[4,4,2,8,128]{4,3,2,1,0:T(8,128)S(1)}, f32[4,4,2,8,128]{4,3,2,1,0:T(8,128)S(1)}, u32[]{:S(2)}, u32[]{:S(2)}) collective-permute-start(f32[4,4,2,8,128]{4,3,2,1,0:T(8,128)S(1)} %get-tuple-element.50), channel_id=1, source_target_pairs={{0,14},{2,12},{4,10},{6,8},{8,6},{10,4},{12,2},{14,0},{1,15},{3,13... | collective-permute-start | bytes 393224 | tf_op jit(solution)/shard_map/ppermute | solution.py:516
  29.4 10.7 %collective-permute-start.18 = (f32[4,4,2,8,128]{4,3,2,1,0:T(8,128)S(1)}, f32[4,4,2,8,128]{4,3,2,1,0:T(8,128)S(1)}, u32[]{:S(2)}, u32[]{:S(2)}) collective-permute-start(f32[4,4,2,8,128]{4,3,2,1,0:T(8,128)S(1)} %get-tuple-element.63), channel_id=1, source_target_pairs={{0,2},{2,0},{4,6},{6,4},{8,10},{10,8},{12,14},{14,12},{1,3},{3,1},... | collective-permute-start | bytes 393224 | tf_op jit(solution)/shard_map/ppermute | solution.py:516
  32.2 11.3 %collective-permute-start.19 = (f32[4,4,2,8,128]{4,3,2,1,0:T(8,128)S(1)}, f32[4,4,2,8,128]{4,3,2,1,0:T(8,128)S(1)}, u32[]{:S(2)}, u32[]{:S(2)}) collective-permute-start(f32[4,4,2,8,128]{4,3,2,1,0:T(8,128)S(1)} %get-tuple-element.64), channel_id=1, source_target_pairs={{0,4},{2,6},{4,0},{6,2},{8,12},{10,14},{12,8},{14,10},{1,5},{3,7},... | collective-permute-start | bytes 393224 | tf_op jit(solution)/shard_map/ppermute | solution.py:516
  32.2 14.7 %collective-permute-start.20 = (f32[4,4,2,8,128]{4,3,2,1,0:T(8,128)S(1)}, f32[4,4,2,8,128]{4,3,2,1,0:T(8,128)S(1)}, u32[]{:S(2)}, u32[]{:S(2)}) collective-permute-start(f32[4,4,2,8,128]{4,3,2,1,0:T(8,128)S(1)} %get-tuple-element.65), channel_id=1, source_target_pairs={{0,6},{2,4},{4,2},{6,0},{8,14},{10,12},{12,10},{14,8},{1,7},{3,5},... | collective-permute-start | bytes 393224 | tf_op jit(solution)/shard_map/ppermute | solution.py:516
  34.7 12.3 %collective-permute-start.21 = (f32[4,4,2,8,128]{4,3,2,1,0:T(8,128)S(1)}, f32[4,4,2,8,128]{4,3,2,1,0:T(8,128)S(1)}, u32[]{:S(2)}, u32[]{:S(2)}) collective-permute-start(f32[4,4,2,8,128]{4,3,2,1,0:T(8,128)S(1)} %get-tuple-element.66), channel_id=1, source_target_pairs={{0,8},{2,10},{4,12},{6,14},{8,0},{10,2},{12,4},{14,6},{1,9},{3,11}... | collective-permute-start | bytes 393224 | tf_op jit(solution)/shard_map/ppermute | solution.py:516
  38.5 8.5 %collective-permute-start.22 = (f32[4,4,2,8,128]{4,3,2,1,0:T(8,128)S(1)}, f32[4,4,2,8,128]{4,3,2,1,0:T(8,128)S(1)}, u32[]{:S(2)}, u32[]{:S(2)}) collective-permute-start(f32[4,4,2,8,128]{4,3,2,1,0:T(8,128)S(1)} %get-tuple-element.67), channel_id=1, source_target_pairs={{0,10},{2,8},{4,14},{6,12},{8,2},{10,0},{12,6},{14,4},{1,11},{3,9}... | collective-permute-start | bytes 393224 | tf_op jit(solution)/shard_map/ppermute | solution.py:516
  40.1 6.9 %collective-permute-start.23 = (f32[4,4,2,8,128]{4,3,2,1,0:T(8,128)S(1)}, f32[4,4,2,8,128]{4,3,2,1,0:T(8,128)S(1)}, u32[]{:S(2)}, u32[]{:S(2)}) collective-permute-start(f32[4,4,2,8,128]{4,3,2,1,0:T(8,128)S(1)} %get-tuple-element.68), channel_id=1, source_target_pairs={{0,12},{2,14},{4,8},{6,10},{8,4},{10,6},{12,0},{14,2},{1,13},{3,15... | collective-permute-start | bytes 393224 | tf_op jit(solution)/shard_map/ppermute | solution.py:516
  43.5 6.8 %collective-permute-start.24 = (f32[4,4,2,8,128]{4,3,2,1,0:T(8,128)S(1)}, f32[4,4,2,8,128]{4,3,2,1,0:T(8,128)S(1)}, u32[]{:S(2)}, u32[]{:S(2)}) collective-permute-start(f32[4,4,2,8,128]{4,3,2,1,0:T(8,128)S(1)} %get-tuple-element.69), channel_id=1, source_target_pairs={{0,14},{2,12},{4,10},{6,8},{8,6},{10,4},{12,2},{14,0},{1,15},{3,13... | collective-permute-start | bytes 393224 | tf_op jit(solution)/shard_map/ppermute | solution.py:516
  46.9 4.2 %collective-permute-start.9 = (f32[16,4096]{1,0:T(8,128)S(1)}, f32[16,4096]{1,0:T(8,128)S(1)}, u32[]{:S(2)}, u32[]{:S(2)}) collective-permute-start(f32[16,4096]{1,0:T(8,128)S(1)} %get-tuple-element.52), channel_id=1, source_target_pairs={{0,1},{1,0},{2,3},{3,2},{4,5},{5,4},{6,7},{7,6},{8,9},{9,8},{10,11... | collective-permute-start | bytes 786440 | tf_op jit(solution)/shard_map/ppermute | solution.py:581
  51.1 21.4 %collective-permute-start.10 = (f32[16,4096]{1,0:T(8,128)S(1)}, f32[16,4096]{1,0:T(8,128)S(1)}, u32[]{:S(2)}, u32[]{:S(2)}) collective-permute-start(f32[16,4096]{1,0:T(8,128)S(1)} %add.74.mine_ref), channel_id=1, source_target_pairs={{0,16},{16,0},{1,17},{17,1},{2,18},{18,2},{3,19},{19,3},{4,20},{20... | collective-permute-start | bytes 786440 | tf_op jit(solution)/shard_map/ppermute | solution.py:582
  54.1 23.8 %collective-permute-start.26 = (f32[16,4096]{1,0:T(8,128)S(1)}, f32[16,4096]{1,0:T(8,128)S(1)}, u32[]{:S(2)}, u32[]{:S(2)}) collective-permute-start(f32[16,4096]{1,0:T(8,128)S(1)} %add.75.mine_ref), channel_id=1, source_target_pairs={{0,16},{16,0},{1,17},{17,1},{2,18},{18,2},{3,19},{19,3},{4,20},{20... | collective-permute-start | bytes 786440 | tf_op jit(solution)/shard_map/ppermute | solution.py:582
  73.3 8.9 %collective-permute-start.11 = (f32[8,2,16,128]{3,2,1,0:T(8,128)S(1)}, f32[8,2,16,128]{3,2,1,0:T(8,128)S(1)}, u32[]{:S(2)}, u32[]{:S(2)}) collective-permute-start(f32[8,2,16,128]{3,2,1,0:T(8,128)S(1)} %bitcast.79), channel_id=1, source_target_pairs={{0,2},{2,0},{4,6},{6,4},{8,10},{10,8},{12,14},{14,12},{1,3},{3,1},... | collective-permute-start | bytes 393224 | tf_op jit(solution)/shard_map/ppermute | solution.py:516
  74.5 8.2 %collective-permute-start.12 = (f32[8,2,16,128]{3,2,1,0:T(8,128)S(1)}, f32[8,2,16,128]{3,2,1,0:T(8,128)S(1)}, u32[]{:S(2)}, u32[]{:S(2)}) collective-permute-start(f32[8,2,16,128]{3,2,1,0:T(8,128)S(1)} %bitcast.77), channel_id=1, source_target_pairs={{0,4},{2,6},{4,0},{6,2},{8,12},{10,14},{12,8},{14,10},{1,5},{3,7},... | collective-permute-start | bytes 393224 | tf_op jit(solution)/shard_map/ppermute | solution.py:516
  78.7 6.4 %collective-permute-start.27 = (f32[8,2,16,128]{3,2,1,0:T(8,128)S(1)}, f32[8,2,16,128]{3,2,1,0:T(8,128)S(1)}, u32[]{:S(2)}, u32[]{:S(2)}) collective-permute-start(f32[8,2,16,128]{3,2,1,0:T(8,128)S(1)} %bitcast.81), channel_id=1, source_target_pairs={{0,2},{2,0},{4,6},{6,4},{8,10},{10,8},{12,14},{14,12},{1,3},{3,1},... | collective-permute-start | bytes 393224 | tf_op jit(solution)/shard_map/ppermute | solution.py:516
  79.7 7.7 %collective-permute-start.28 = (f32[8,2,16,128]{3,2,1,0:T(8,128)S(1)}, f32[8,2,16,128]{3,2,1,0:T(8,128)S(1)}, u32[]{:S(2)}, u32[]{:S(2)}) collective-permute-start(f32[8,2,16,128]{3,2,1,0:T(8,128)S(1)} %bitcast.80), channel_id=1, source_target_pairs={{0,4},{2,6},{4,0},{6,2},{8,12},{10,14},{12,8},{14,10},{1,5},{3,7},... | collective-permute-start | bytes 393224 | tf_op jit(solution)/shard_map/ppermute | solution.py:516
  80.3 7.8 %collective-permute-start.29 = (f32[8,2,16,128]{3,2,1,0:T(8,128)S(1)}, f32[8,2,16,128]{3,2,1,0:T(8,128)S(1)}, u32[]{:S(2)}, u32[]{:S(2)}) collective-permute-start(f32[8,2,16,128]{3,2,1,0:T(8,128)S(1)} %bitcast.78), channel_id=1, source_target_pairs={{0,6},{2,4},{4,2},{6,0},{8,14},{10,12},{12,10},{14,8},{1,7},{3,5},... | collective-permute-start | bytes 393224 | tf_op jit(solution)/shard_map/ppermute | solution.py:516
  82.3 7.5 %collective-permute-start.30 = (f32[8,2,16,128]{3,2,1,0:T(8,128)S(1)}, f32[8,2,16,128]{3,2,1,0:T(8,128)S(1)}, u32[]{:S(2)}, u32[]{:S(2)}) collective-permute-start(f32[8,2,16,128]{3,2,1,0:T(8,128)S(1)} %bitcast.76), channel_id=1, source_target_pairs={{0,8},{2,10},{4,12},{6,14},{8,0},{10,2},{12,4},{14,6},{1,9},{3,11}... | collective-permute-start | bytes 393224 | tf_op jit(solution)/shard_map/ppermute | solution.py:516
  82.7 9.2 %collective-permute-start.31 = (f32[8,2,16,128]{3,2,1,0:T(8,128)S(1)}, f32[8,2,16,128]{3,2,1,0:T(8,128)S(1)}, u32[]{:S(2)}, u32[]{:S(2)}) collective-permute-start(f32[8,2,16,128]{3,2,1,0:T(8,128)S(1)} %bitcast.75), channel_id=1, source_target_pairs={{0,10},{2,8},{4,14},{6,12},{8,2},{10,0},{12,6},{14,4},{1,11},{3,9}... | collective-permute-start | bytes 393224 | tf_op jit(solution)/shard_map/ppermute | solution.py:516
  85.1 9.2 %collective-permute-start.32 = (f32[8,2,16,128]{3,2,1,0:T(8,128)S(1)}, f32[8,2,16,128]{3,2,1,0:T(8,128)S(1)}, u32[]{:S(2)}, u32[]{:S(2)}) collective-permute-start(f32[8,2,16,128]{3,2,1,0:T(8,128)S(1)} %bitcast.74), channel_id=1, source_target_pairs={{0,12},{2,14},{4,8},{6,10},{8,4},{10,6},{12,0},{14,2},{1,13},{3,15... | collective-permute-start | bytes 393224 | tf_op jit(solution)/shard_map/ppermute | solution.py:516
  87.3 10.2 %collective-permute-start.33 = (f32[8,2,16,128]{3,2,1,0:T(8,128)S(1)}, f32[8,2,16,128]{3,2,1,0:T(8,128)S(1)}, u32[]{:S(2)}, u32[]{:S(2)}) collective-permute-start(f32[8,2,16,128]{3,2,1,0:T(8,128)S(1)} %bitcast.73), channel_id=1, source_target_pairs={{0,14},{2,12},{4,10},{6,8},{8,6},{10,4},{12,2},{14,0},{1,15},{3,13... | collective-permute-start | bytes 393224 | tf_op jit(solution)/shard_map/ppermute | solution.py:516
  88.1 12.9 %collective-permute-start.13 = (f32[8,2,16,128]{3,2,1,0:T(8,128)S(1)}, f32[8,2,16,128]{3,2,1,0:T(8,128)S(1)}, u32[]{:S(2)}, u32[]{:S(2)}) collective-permute-start(f32[8,2,16,128]{3,2,1,0:T(8,128)S(1)} %bitcast.72), channel_id=1, source_target_pairs={{0,6},{2,4},{4,2},{6,0},{8,14},{10,12},{12,10},{14,8},{1,7},{3,5},... | collective-permute-start | bytes 393224 | tf_op jit(solution)/shard_map/ppermute | solution.py:516
  89.7 11.3 %collective-permute-start.14 = (f32[8,2,16,128]{3,2,1,0:T(8,128)S(1)}, f32[8,2,16,128]{3,2,1,0:T(8,128)S(1)}, u32[]{:S(2)}, u32[]{:S(2)}) collective-permute-start(f32[8,2,16,128]{3,2,1,0:T(8,128)S(1)} %bitcast.71), channel_id=1, source_target_pairs={{0,8},{2,10},{4,12},{6,14},{8,0},{10,2},{12,4},{14,6},{1,9},{3,11}... | collective-permute-start | bytes 393224 | tf_op jit(solution)/shard_map/ppermute | solution.py:516
  91.9 11.1 %collective-permute-start.15 = (f32[8,2,16,128]{3,2,1,0:T(8,128)S(1)}, f32[8,2,16,128]{3,2,1,0:T(8,128)S(1)}, u32[]{:S(2)}, u32[]{:S(2)}) collective-permute-start(f32[8,2,16,128]{3,2,1,0:T(8,128)S(1)} %bitcast.70), channel_id=1, source_target_pairs={{0,10},{2,8},{4,14},{6,12},{8,2},{10,0},{12,6},{14,4},{1,11},{3,9}... | collective-permute-start | bytes 393224 | tf_op jit(solution)/shard_map/ppermute | solution.py:516
  94.3 10.5 %collective-permute-start.16 = (f32[8,2,16,128]{3,2,1,0:T(8,128)S(1)}, f32[8,2,16,128]{3,2,1,0:T(8,128)S(1)}, u32[]{:S(2)}, u32[]{:S(2)}) collective-permute-start(f32[8,2,16,128]{3,2,1,0:T(8,128)S(1)} %bitcast.69), channel_id=1, source_target_pairs={{0,12},{2,14},{4,8},{6,10},{8,4},{10,6},{12,0},{14,2},{1,13},{3,15... | collective-permute-start | bytes 393224 | tf_op jit(solution)/shard_map/ppermute | solution.py:516
  97.5 9.2 %collective-permute-start.17 = (f32[8,2,16,128]{3,2,1,0:T(8,128)S(1)}, f32[8,2,16,128]{3,2,1,0:T(8,128)S(1)}, u32[]{:S(2)}, u32[]{:S(2)}) collective-permute-start(f32[8,2,16,128]{3,2,1,0:T(8,128)S(1)} %bitcast.68), channel_id=1, source_target_pairs={{0,14},{2,12},{4,10},{6,8},{8,6},{10,4},{12,2},{14,0},{1,15},{3,13... | collective-permute-start | bytes 393224 | tf_op jit(solution)/shard_map/ppermute | solution.py:516
  (10 other events, 79.0 us)

commit v2 on v1

--- a/solution.py
+++ b/solution.py
@@ -92,7 +92,8 @@
     side = obj.shape[3]
     lead = table_ref[0] >> (2 * side.bit_length() - 2 + spots.bit_length())
     local = o_re.shape[0]
-    first, me = lead & (local - 1), lead >> (local.bit_length() - 1)
+    first, place_of = lead & (local - 1), lead >> (local.bit_length() - 1)
+    me, far = place_of & (dests - 1), place_of >> (dests.bit_length() - 1)
     sums = (sum_re, sum_im, sum_light)
 
     def in_copies(e):
@@ -271,7 +272,9 @@
 
         def finish(k, carry):
             for d in range(dests):
-                n = ((k >> (tiles.bit_length() - 1)) * dests + (d ^ me)) * tiles + (k & (tiles - 1))
+                f = k >> (tiles.bit_length() - 1)
+                across = jnp.where(f == far, 0, dests // 2) if dests > 1 else 0
+                n = (f * dests + (d ^ me ^ across)) * tiles + (k & (tiles - 1))
                 at = pl.ds(pl.multiple_of(n * SUBS, SUBS), SUBS)
                 mid = [pltpu.roll(acc[2, at, :], LANES // 2, 1) for acc in sums]
                 for h in range(2):
@@ -369,7 +372,7 @@
         column = gram[:, k:k + 1]
         gram = jnp.where(row == k, line, gram - column * line)
         right = jnp.where(row == k, rhs, right - column * rhs)
-    far, me, tile = where_ref[0], where_ref[1], where_ref[2]
+    me, far, tile = where_ref[0], where_ref[1], where_ref[2]
     both = 2 * n_e
 
     def chosen(shape, axis, per, offset):
@@ -482,8 +485,13 @@
 def gather_kernel(part, senders, me_ref, *refs):
     got, (out_ref, sem) = refs[:senders], refs[-2:]
     copies = [
-        pltpu.make_async_copy(ref, out_ref.at[part, :, :, me_ref[0] ^ d], sem.at[d])
+        pltpu.make_async_copy(
+            ref.at[:, f],
+            out_ref.at[part, :, f, me_ref[0] ^ d ^ jnp.where(me_ref[1] == f, 0, senders // 2)],
+            sem.at[d, f],
+        )
         for d, ref in enumerate(got)
+        for f in range(ref.shape[1])
     ]
     for c in copies:
         c.start()
@@ -503,7 +511,7 @@
         + [pl.BlockSpec(memory_space=pltpu.VMEM)] * senders
         + ([] if out is None else [hbm]),
         out_specs=hbm,
-        scratch_shapes=[pltpu.SemaphoreType.DMA((senders,))],
+        scratch_shapes=[pltpu.SemaphoreType.DMA((senders, fars))],
         input_output_aliases={} if out is None else {1 + senders: 0},
         compiler_params=pltpu.CompilerParams(vmem_limit_bytes=SMALL),
         name="gather_part",
@@ -549,7 +557,7 @@
     par_rec = lax.ppermute(give, "ta", swap)
     table = slot_table(
         window_corners[:, 0], theirs[:, 0], filled_tallies, first.astype(jnp.int32), n_e, side,
-        lax.axis_index("cube").astype(jnp.int32) if two_level else 0,
+        (lax.axis_index("far") * cube + lax.axis_index("cube")).astype(jnp.int32) if two_level else 0,
     )
     stepped = gradient_step(
         (sample_inphase, sample_quadrature),
@@ -566,8 +574,11 @@
     if two_level:
         far = lax.axis_index("far").astype(jnp.int32)
         me = lax.axis_index("cube").astype(jnp.int32)
-        where = jnp.stack([far, me, tile.astype(jnp.int32)])
+        where = jnp.stack([me, far, tile.astype(jnp.int32)])
         project_near, basis_near = solve_templates(where, absorption_templates, fars, cube, n_e)
+        opposite = [
+            (f * cube + c, (1 - f) * cube + (c ^ (cube // 2))) for f in range(2) for c in range(cube)
+        ]
         out, coefs = None, []
         parts = stepped[:cube], stepped[cube:]
         got = []
@@ -579,12 +590,12 @@
                 tile.astype(jnp.int32)[None], project_near, blocks, fars, tiles
             )
             share = kept + lax.ppermute(given, "ta", swap)
-            theirs = lax.ppermute(share, "far", swap)
+            theirs = lax.ppermute(share, ("far", "cube"), opposite)
             coef, fit = fitted_values(far[None], share, theirs, basis_near, pix, cube)
             coefs.append(coef)
             fit = [x.reshape(local_energies, fars, pix // LANES, LANES) for x in fit]
             back = exchange(fit, cube)
-            out = gather_part(part, me[None], back, out)
+            out = gather_part(part, where[:2], back, out)
         return (out.reshape(2, local_energies, cube * fars, 1, pix), jnp.stack(coefs))
 
     gram = jnp.dot(absorption_templates, absorption_templates.T, precision=HIGHEST)

time: 108 us -> 106 us (0.981)
  waiting for transfers between devices: 43.2 us -> 24 us
  starting transfers between devices: 42.1 us -> 58.9 us
  Pallas kernels: 17.9 us -> 19.2 us
    ppermute x28, starting transfers between devices: 36.9 us -> 53.1 us  [exchange(): got[d] = lax.ppermute(blocks[d], 'cube', [(i, i ^ d) for i in range(cube)])]
    ppermute x2, waiting for transfers between devices: 19.8 us -> 8.63 us  [local(): theirs = lax.ppermute(share, ('far', 'cube'), opposite)]
    ppermute x28, waiting for transfers between devices: 21 us -> 13.3 us  [exchange(): got[d] = lax.ppermute(blocks[d], 'cube', [(i, i ^ d) for i in range(cube)])]
    pallas_call x2, Pallas kernels: 2.05 us -> 3.27 us  [gather_part(): pl.pallas_call(functools.partial(gather_kernel, part, senders), out_shape...]
  transfers between devices with their start and end apart: 34 -> 34, of which waited for: 16 -> 10; matrix products, arithmetic and copies ran while one was open for 3% -> 3% of each run, Pallas kernels for 6% -> 7%
where the time goes in v2:
time: 106 us
  starting transfers between devices  58.9 us (56%)
  waiting for transfers between devices  24 us (23%)
  Pallas kernels  19.2 us (18%)
  local copies, waits for them, and re-layouts  1.42 us (1%)
  other arithmetic  1.39 us (1%)
    ppermute x28, starting transfers between devices, exchange(): got[d] = lax.ppermute(blocks[d], 'cube', [(i, i ^ d) for i in range(cube)])  53.1 us
    ppermute x28, waiting for transfers between devices, exchange(): got[d] = lax.ppermute(blocks[d], 'cube', [(i, i ^ d) for i in range(cube)])  13.3 us
    pallas_call x1, Pallas kernels, gradient_step(): pl.pallas_call(functools.partial(step_kernel, n_e, spots, used, modes, wi...  10.7 us
    ppermute x2, waiting for transfers between devices, local(): theirs = lax.ppermute(share, ('far', 'cube'), opposite)  8.63 us
    ppermute x2, starting transfers between devices, local(): theirs = lax.ppermute(share, ('far', 'cube'), opposite)  4.97 us
    pallas_call x2, Pallas kernels, gather_part(): pl.pallas_call(functools.partial(gather_kernel, part, senders), out_shape...  3.27 us
  transfers between devices with their start and end apart: 34, of which 10 were waited for; matrix products, arithmetic and copies ran while one was open for 3% of the time, Pallas kernels for 7%

profile of v2, /device:TPU:0, one launch (start us, length us, event | category | flops | bytes accessed | tf_op | source)
XLA Modules:
  0.0 105.8 jit_solution(725008479182495672)
XLA Ops:
  1.3 1.3 %dynamic-slice_bitcast_fusion = f32[4,16,32,32]{3,2,1,0:T(8,128)S(1)} fusion(f32[8,1,16,32,32]{4,3,2,1,0:T(8,128)} %param.15, s32[]{:T(128)S(6)} %select_n.22), kind=kLoop, calls=%fused_computation | loop fusion | bytes 524292 | tf_op jit(solution)/shard_map/dynamic_slice | solution.py:556
  3.3 2.1 %collective-permute-done.1.par_rec = f32[4,16,32,32]{3,2,1,0:T(8,128)} collective-permute-done((f32[4,16,32,32]{3,2,1,0:T(8,128)S(1)}, f32[4,16,32,32]{3,2,1,0:T(8,128)}, u32[]{:S(2)}, u32[]{:S(2)}) %collective-permute-start.1) | collective-permute-done | bytes 262176 | tf_op jit(solution)/shard_map/ppermute | solution.py:557
  5.5 10.7 %gradient_step.1 = (f32[4,4,2,8,128]{4,3,2,1,0:T(8,128)S(1)}, f32[4,4,2,8,128]{4,3,2,1,0:T(8,128)S(1)}, f32[4,4,2,8,128]{4,3,2,1,0:T(8,128)S(1)}, f32[4,4,2,8,12...) custom-call(s32[96]{0:T(128)S(1)} %reshape.182.table_ref, ...), custom_call_target="tpu_custom_call" | custom-call | tf_op jit(solution)/shard_map/gradient_step/pallas_call | solution.py:304
  16.1 2.7 %collective-permute-start.2 = (f32[4,4,2,8,128]{4,3,2,1,0:T(8,128)S(1)}, f32[4,4,2,8,128]{4,3,2,1,0:T(8,128)S(1)}, u32[]{:S(2)}, u32[]{:S(2)}) collective-permute-start(f32[4,4,2,8,128]{4,3,2,1,0:T(8,128)S(1)} %get-tuple-element.44), channel_id=1, source_target_pairs={{0,2},{2,0},{4,6},{6,4},{8,10},{10,8},{12,14},{14,12},{1,3},{3,1},... | collective-permute-start | bytes 393224 | tf_op jit(solution)/shard_map/ppermute | solution.py:524
  18.8 1.5 %collective-permute-start.3 = (f32[4,4,2,8,128]{4,3,2,1,0:T(8,128)S(1)}, f32[4,4,2,8,128]{4,3,2,1,0:T(8,128)S(1)}, u32[]{:S(2)}, u32[]{:S(2)}) collective-permute-start(f32[4,4,2,8,128]{4,3,2,1,0:T(8,128)S(1)} %get-tuple-element.45), channel_id=1, source_target_pairs={{0,4},{2,6},{4,0},{6,2},{8,12},{10,14},{12,8},{14,10},{1,5},{3,7},... | collective-permute-start | bytes 393224 | tf_op jit(solution)/shard_map/ppermute | solution.py:524
  20.3 2.0 %collective-permute-start.5 = (f32[4,4,2,8,128]{4,3,2,1,0:T(8,128)S(1)}, f32[4,4,2,8,128]{4,3,2,1,0:T(8,128)S(1)}, u32[]{:S(2)}, u32[]{:S(2)}) collective-permute-start(f32[4,4,2,8,128]{4,3,2,1,0:T(8,128)S(1)} %get-tuple-element.47), channel_id=1, source_target_pairs={{0,8},{2,10},{4,12},{6,14},{8,0},{10,2},{12,4},{14,6},{1,9},{3,11}... | collective-permute-start | bytes 393224 | tf_op jit(solution)/shard_map/ppermute | solution.py:524
  22.4 1.4 %collective-permute-start.6 = (f32[4,4,2,8,128]{4,3,2,1,0:T(8,128)S(1)}, f32[4,4,2,8,128]{4,3,2,1,0:T(8,128)S(1)}, u32[]{:S(2)}, u32[]{:S(2)}) collective-permute-start(f32[4,4,2,8,128]{4,3,2,1,0:T(8,128)S(1)} %get-tuple-element.48), channel_id=1, source_target_pairs={{0,10},{2,8},{4,14},{6,12},{8,2},{10,0},{12,6},{14,4},{1,11},{3,9}... | collective-permute-start | bytes 393224 | tf_op jit(solution)/shard_map/ppermute | solution.py:524
  23.7 2.5 %collective-permute-start.7 = (f32[4,4,2,8,128]{4,3,2,1,0:T(8,128)S(1)}, f32[4,4,2,8,128]{4,3,2,1,0:T(8,128)S(1)}, u32[]{:S(2)}, u32[]{:S(2)}) collective-permute-start(f32[4,4,2,8,128]{4,3,2,1,0:T(8,128)S(1)} %get-tuple-element.49), channel_id=1, source_target_pairs={{0,12},{2,14},{4,8},{6,10},{8,4},{10,6},{12,0},{14,2},{1,13},{3,15... | collective-permute-start | bytes 393224 | tf_op jit(solution)/shard_map/ppermute | solution.py:524
  26.6 1.7 %collective-permute-start.8 = (f32[4,4,2,8,128]{4,3,2,1,0:T(8,128)S(1)}, f32[4,4,2,8,128]{4,3,2,1,0:T(8,128)S(1)}, u32[]{:S(2)}, u32[]{:S(2)}) collective-permute-start(f32[4,4,2,8,128]{4,3,2,1,0:T(8,128)S(1)} %get-tuple-element.50), channel_id=1, source_target_pairs={{0,14},{2,12},{4,10},{6,8},{8,6},{10,4},{12,2},{14,0},{1,15},{3,13... | collective-permute-start | bytes 393224 | tf_op jit(solution)/shard_map/ppermute | solution.py:524
  28.3 2.9 %collective-permute-start.18 = (f32[4,4,2,8,128]{4,3,2,1,0:T(8,128)S(1)}, f32[4,4,2,8,128]{4,3,2,1,0:T(8,128)S(1)}, u32[]{:S(2)}, u32[]{:S(2)}) collective-permute-start(f32[4,4,2,8,128]{4,3,2,1,0:T(8,128)S(1)} %get-tuple-element.63), channel_id=1, source_target_pairs={{0,2},{2,0},{4,6},{6,4},{8,10},{10,8},{12,14},{14,12},{1,3},{3,1},... | collective-permute-start | bytes 393224 | tf_op jit(solution)/shard_map/ppermute | solution.py:524
  31.2 1.5 %collective-permute-start.20 = (f32[4,4,2,8,128]{4,3,2,1,0:T(8,128)S(1)}, f32[4,4,2,8,128]{4,3,2,1,0:T(8,128)S(1)}, u32[]{:S(2)}, u32[]{:S(2)}) collective-permute-start(f32[4,4,2,8,128]{4,3,2,1,0:T(8,128)S(1)} %get-tuple-element.65), channel_id=1, source_target_pairs={{0,6},{2,4},{4,2},{6,0},{8,14},{10,12},{12,10},{14,8},{1,7},{3,5},... | collective-permute-start | bytes 393224 | tf_op jit(solution)/shard_map/ppermute | solution.py:524
  33.6 1.9 %collective-permute-start.21 = (f32[4,4,2,8,128]{4,3,2,1,0:T(8,128)S(1)}, f32[4,4,2,8,128]{4,3,2,1,0:T(8,128)S(1)}, u32[]{:S(2)}, u32[]{:S(2)}) collective-permute-start(f32[4,4,2,8,128]{4,3,2,1,0:T(8,128)S(1)} %get-tuple-element.66), channel_id=1, source_target_pairs={{0,8},{2,10},{4,12},{6,14},{8,0},{10,2},{12,4},{14,6},{1,9},{3,11}... | collective-permute-start | bytes 393224 | tf_op jit(solution)/shard_map/ppermute | solution.py:524
  35.5 2.0 %collective-permute-done.8 = f32[4,4,2,8,128]{4,3,2,1,0:T(8,128)S(1)} collective-permute-done((f32[4,4,2,8,128]{4,3,2,1,0:T(8,128)S(1)}, f32[4,4,2,8,128]{4,3,2,1,0:T(8,128)S(1)}, u32[]{:S(2)}, u32[]{:S(2)}) %collective-permute-start.8) | collective-permute-done | bytes 131104 | tf_op jit(solution)/shard_map/ppermute | solution.py:524
  37.4 1.6 %collective-permute-start.22 = (f32[4,4,2,8,128]{4,3,2,1,0:T(8,128)S(1)}, f32[4,4,2,8,128]{4,3,2,1,0:T(8,128)S(1)}, u32[]{:S(2)}, u32[]{:S(2)}) collective-permute-start(f32[4,4,2,8,128]{4,3,2,1,0:T(8,128)S(1)} %get-tuple-element.67), channel_id=1, source_target_pairs={{0,10},{2,8},{4,14},{6,12},{8,2},{10,0},{12,6},{14,4},{1,11},{3,9}... | collective-permute-start | bytes 393224 | tf_op jit(solution)/shard_map/ppermute | solution.py:524
  39.1 3.4 %collective-permute-done.19 = f32[4,4,2,8,128]{4,3,2,1,0:T(8,128)S(1)} collective-permute-done((f32[4,4,2,8,128]{4,3,2,1,0:T(8,128)S(1)}, f32[4,4,2,8,128]{4,3,2,1,0:T(8,128)S(1)}, u32[]{:S(2)}, u32[]{:S(2)}) %collective-permute-start.19) | collective-permute-done | bytes 131104 | tf_op jit(solution)/shard_map/ppermute | solution.py:524
  42.9 2.1 %solve_templates.1 = (f32[16,32]{1,0:T(8,128)S(1)}, f32[64,16]{1,0:T(8,128)S(1)}) custom-call(s32[3]{0:T(128)S(1)} %pad_add_fusion.1.where_ref, f32[16,128]{1,0:T(8,128)S(1)} %copy-done.4), custom_call_target="tpu_custom_call" | custom-call | tf_op jit(solution)/shard_map/solve_templates/pallas_call | solution.py:395
  45.9 3.3 %collective-permute-done.24 = f32[4,4,2,8,128]{4,3,2,1,0:T(8,128)S(1)} collective-permute-done((f32[4,4,2,8,128]{4,3,2,1,0:T(8,128)S(1)}, f32[4,4,2,8,128]{4,3,2,1,0:T(8,128)S(1)}, u32[]{:S(2)}, u32[]{:S(2)}) %collective-permute-start.24) | collective-permute-done | bytes 131104 | tf_op jit(solution)/shard_map/ppermute | solution.py:524
  50.1 3.5 %collective-permute-start.10 = (f32[16,4096]{1,0:T(8,128)S(1)}, f32[16,4096]{1,0:T(8,128)S(1)}, u32[]{:S(2)}, u32[]{:S(2)}) collective-permute-start(f32[16,4096]{1,0:T(8,128)S(1)} %add.78.mine_ref), channel_id=1, source_target_pairs={{0,24},{2,26},{4,28},{6,30},{8,16},{10,18},{12,20},{14,22},{16,8},... | collective-permute-start | bytes 786440 | tf_op jit(solution)/shard_map/ppermute | solution.py:593
  53.6 1.5 %collective-permute-start.26 = (f32[16,4096]{1,0:T(8,128)S(1)}, f32[16,4096]{1,0:T(8,128)S(1)}, u32[]{:S(2)}, u32[]{:S(2)}) collective-permute-start(f32[16,4096]{1,0:T(8,128)S(1)} %add.79.mine_ref), channel_id=1, source_target_pairs={{0,24},{2,26},{4,28},{6,30},{8,16},{10,18},{12,20},{14,22},{16,8},... | collective-permute-start | bytes 786440 | tf_op jit(solution)/shard_map/ppermute | solution.py:593
  55.1 6.1 %collective-permute-done.10.theirs_ref = f32[16,4096]{1,0:T(8,128)S(1)} collective-permute-done((f32[16,4096]{1,0:T(8,128)S(1)}, f32[16,4096]{1,0:T(8,128)S(1)}, u32[]{:S(2)}, u32[]{:S(2)}) %collective-permute-start.10) | collective-permute-done | bytes 262176 | tf_op jit(solution)/shard_map/ppermute | solution.py:593
  63.9 2.5 %collective-permute-done.26.theirs_ref = f32[16,4096]{1,0:T(8,128)S(1)} collective-permute-done((f32[16,4096]{1,0:T(8,128)S(1)}, f32[16,4096]{1,0:T(8,128)S(1)}, u32[]{:S(2)}, u32[]{:S(2)}) %collective-permute-start.26) | collective-permute-done | bytes 262176 | tf_op jit(solution)/shard_map/ppermute | solution.py:593
  69.0 1.7 %collective-permute-start.29 = (f32[8,2,16,128]{3,2,1,0:T(8,128)S(1)}, f32[8,2,16,128]{3,2,1,0:T(8,128)S(1)}, u32[]{:S(2)}, u32[]{:S(2)}) collective-permute-start(f32[8,2,16,128]{3,2,1,0:T(8,128)S(1)} %bitcast.77), channel_id=1, source_target_pairs={{0,6},{2,4},{4,2},{6,0},{8,14},{10,12},{12,10},{14,8},{1,7},{3,5},... | collective-permute-start | bytes 393224 | tf_op jit(solution)/shard_map/ppermute | solution.py:524
  70.7 11.0 %collective-permute-start.30 = (f32[8,2,16,128]{3,2,1,0:T(8,128)S(1)}, f32[8,2,16,128]{3,2,1,0:T(8,128)S(1)}, u32[]{:S(2)}, u32[]{:S(2)}) collective-permute-start(f32[8,2,16,128]{3,2,1,0:T(8,128)S(1)} %bitcast.76), channel_id=1, source_target_pairs={{0,8},{2,10},{4,12},{6,14},{8,0},{10,2},{12,4},{14,6},{1,9},{3,11}... | collective-permute-start | bytes 393224 | tf_op jit(solution)/shard_map/ppermute | solution.py:524
  82.1 1.4 %collective-permute-start.32 = (f32[8,2,16,128]{3,2,1,0:T(8,128)S(1)}, f32[8,2,16,128]{3,2,1,0:T(8,128)S(1)}, u32[]{:S(2)}, u32[]{:S(2)}) collective-permute-start(f32[8,2,16,128]{3,2,1,0:T(8,128)S(1)} %bitcast.74), channel_id=1, source_target_pairs={{0,12},{2,14},{4,8},{6,10},{8,4},{10,6},{12,0},{14,2},{1,13},{3,15... | collective-permute-start | bytes 393224 | tf_op jit(solution)/shard_map/ppermute | solution.py:524
  83.5 2.8 %collective-permute-start.33 = (f32[8,2,16,128]{3,2,1,0:T(8,128)S(1)}, f32[8,2,16,128]{3,2,1,0:T(8,128)S(1)}, u32[]{:S(2)}, u32[]{:S(2)}) collective-permute-start(f32[8,2,16,128]{3,2,1,0:T(8,128)S(1)} %bitcast.73), channel_id=1, source_target_pairs={{0,14},{2,12},{4,10},{6,8},{8,6},{10,4},{12,2},{14,0},{1,15},{3,13... | collective-permute-start | bytes 393224 | tf_op jit(solution)/shard_map/ppermute | solution.py:524
  86.4 3.4 %collective-permute-start.13 = (f32[8,2,16,128]{3,2,1,0:T(8,128)S(1)}, f32[8,2,16,128]{3,2,1,0:T(8,128)S(1)}, u32[]{:S(2)}, u32[]{:S(2)}) collective-permute-start(f32[8,2,16,128]{3,2,1,0:T(8,128)S(1)} %bitcast.72), channel_id=1, source_target_pairs={{0,6},{2,4},{4,2},{6,0},{8,14},{10,12},{12,10},{14,8},{1,7},{3,5},... | collective-permute-start | bytes 393224 | tf_op jit(solution)/shard_map/ppermute | solution.py:524
  89.8 2.1 %collective-permute-start.15 = (f32[8,2,16,128]{3,2,1,0:T(8,128)S(1)}, f32[8,2,16,128]{3,2,1,0:T(8,128)S(1)}, u32[]{:S(2)}, u32[]{:S(2)}) collective-permute-start(f32[8,2,16,128]{3,2,1,0:T(8,128)S(1)} %bitcast.70), channel_id=1, source_target_pairs={{0,10},{2,8},{4,14},{6,12},{8,2},{10,0},{12,6},{14,4},{1,11},{3,9}... | collective-permute-start | bytes 393224 | tf_op jit(solution)/shard_map/ppermute | solution.py:524
  91.9 3.5 %collective-permute-start.16 = (f32[8,2,16,128]{3,2,1,0:T(8,128)S(1)}, f32[8,2,16,128]{3,2,1,0:T(8,128)S(1)}, u32[]{:S(2)}, u32[]{:S(2)}) collective-permute-start(f32[8,2,16,128]{3,2,1,0:T(8,128)S(1)} %bitcast.69), channel_id=1, source_target_pairs={{0,12},{2,14},{4,8},{6,10},{8,4},{10,6},{12,0},{14,2},{1,13},{3,15... | collective-permute-start | bytes 393224 | tf_op jit(solution)/shard_map/ppermute | solution.py:524
  95.4 2.9 %collective-permute-start.17 = (f32[8,2,16,128]{3,2,1,0:T(8,128)S(1)}, f32[8,2,16,128]{3,2,1,0:T(8,128)S(1)}, u32[]{:S(2)}, u32[]{:S(2)}) collective-permute-start(f32[8,2,16,128]{3,2,1,0:T(8,128)S(1)} %bitcast.68), channel_id=1, source_target_pairs={{0,14},{2,12},{4,10},{6,8},{8,6},{10,4},{12,2},{14,0},{1,15},{3,13... | collective-permute-start | bytes 393224 | tf_op jit(solution)/shard_map/ppermute | solution.py:524
  99.1 1.6 %gather_part.2.refs_8_ = f32[2,8,2,8,16,128]{5,4,3,2,1,0:T(8,128)} custom-call(s32[2]{0:T(128)S(1)} %pad_add_fusion.me_ref, f32[8,2,16,128]{3,2,1,0:T(8,128)S(1)} %bitcast.67, f32[8,2,16,128]{3,2,1,0:T(8,128)S(1)} %collective-permute-done.27.refs_1_, f32[8,2,16,128]{3,2,1,0:T(8,128)S(1)} %collective-permute-done.28.refs_2_, ...), custom_call_target="tpu_custom_call" | custom-call | tf_op jit(solution)/shard_map/gather_part/pallas_call | solution.py:507
  102.0 2.2 %collective-permute-done.17.refs_7_ = f32[8,2,16,128]{3,2,1,0:T(8,128)S(1)} collective-permute-done((f32[8,2,16,128]{3,2,1,0:T(8,128)S(1)}, f32[8,2,16,128]{3,2,1,0:T(8,128)S(1)}, u32[]{:S(2)}, u32[]{:S(2)}) %collective-permute-start.17) | collective-permute-done | bytes 131104 | tf_op jit(solution)/shard_map/ppermute | solution.py:524
  104.1 1.6 %gather_part.3 = f32[2,8,2,8,16,128]{5,4,3,2,1,0:T(8,128)} custom-call(s32[2]{0:T(128)S(1)} %pad_add_fusion.me_ref, f32[8,2,16,128]{3,2,1,0:T(8,128)S(1)} %bitcast.48, f32[8,2,16,128]{3,2,1,0:T(8,128)S(1)} %collective-permute-done.11.refs_1_, f32[8,2,16,128]{3,2,1,0:T(8,128)S(1)} %collective-permute-done.12.refs_2_, ...), custom_call_target="tpu_custom_call", output_to_operand_aliasing={{}: (9, {})} | custom-call | tf_op jit(solution)/shard_map/gather_part/pallas_call | solution.py:507
  (74 shorter events, 12.5 us)
Async XLA Ops:
  16.1 7.6 %collective-permute-start.2 = (f32[4,4,2,8,128]{4,3,2,1,0:T(8,128)S(1)}, f32[4,4,2,8,128]{4,3,2,1,0:T(8,128)S(1)}, u32[]{:S(2)}, u32[]{:S(2)}) collective-permute-start(f32[4,4,2,8,128]{4,3,2,1,0:T(8,128)S(1)} %get-tuple-element.44), channel_id=1, source_target_pairs={{0,2},{2,0},{4,6},{6,4},{8,10},{10,8},{12,14},{14,12},{1,3},{3,1},... | collective-permute-start | bytes 393224 | tf_op jit(solution)/shard_map/ppermute | solution.py:524
  18.8 7.8 %collective-permute-start.3 = (f32[4,4,2,8,128]{4,3,2,1,0:T(8,128)S(1)}, f32[4,4,2,8,128]{4,3,2,1,0:T(8,128)S(1)}, u32[]{:S(2)}, u32[]{:S(2)}) collective-permute-start(f32[4,4,2,8,128]{4,3,2,1,0:T(8,128)S(1)} %get-tuple-element.45), channel_id=1, source_target_pairs={{0,4},{2,6},{4,0},{6,2},{8,12},{10,14},{12,8},{14,10},{1,5},{3,7},... | collective-permute-start | bytes 393224 | tf_op jit(solution)/shard_map/ppermute | solution.py:524
  20.3 8.0 %collective-permute-start.4 = (f32[4,4,2,8,128]{4,3,2,1,0:T(8,128)S(1)}, f32[4,4,2,8,128]{4,3,2,1,0:T(8,128)S(1)}, u32[]{:S(2)}, u32[]{:S(2)}) collective-permute-start(f32[4,4,2,8,128]{4,3,2,1,0:T(8,128)S(1)} %get-tuple-element.46), channel_id=1, source_target_pairs={{0,6},{2,4},{4,2},{6,0},{8,14},{10,12},{12,10},{14,8},{1,7},{3,5},... | collective-permute-start | bytes 393224 | tf_op jit(solution)/shard_map/ppermute | solution.py:524
  20.3 10.8 %collective-permute-start.5 = (f32[4,4,2,8,128]{4,3,2,1,0:T(8,128)S(1)}, f32[4,4,2,8,128]{4,3,2,1,0:T(8,128)S(1)}, u32[]{:S(2)}, u32[]{:S(2)}) collective-permute-start(f32[4,4,2,8,128]{4,3,2,1,0:T(8,128)S(1)} %get-tuple-element.47), channel_id=1, source_target_pairs={{0,8},{2,10},{4,12},{6,14},{8,0},{10,2},{12,4},{14,6},{1,9},{3,11}... | collective-permute-start | bytes 393224 | tf_op jit(solution)/shard_map/ppermute | solution.py:524
  22.4 8.8 %collective-permute-start.6 = (f32[4,4,2,8,128]{4,3,2,1,0:T(8,128)S(1)}, f32[4,4,2,8,128]{4,3,2,1,0:T(8,128)S(1)}, u32[]{:S(2)}, u32[]{:S(2)}) collective-permute-start(f32[4,4,2,8,128]{4,3,2,1,0:T(8,128)S(1)} %get-tuple-element.48), channel_id=1, source_target_pairs={{0,10},{2,8},{4,14},{6,12},{8,2},{10,0},{12,6},{14,4},{1,11},{3,9}... | collective-permute-start | bytes 393224 | tf_op jit(solution)/shard_map/ppermute | solution.py:524
  23.7 9.8 %collective-permute-start.7 = (f32[4,4,2,8,128]{4,3,2,1,0:T(8,128)S(1)}, f32[4,4,2,8,128]{4,3,2,1,0:T(8,128)S(1)}, u32[]{:S(2)}, u32[]{:S(2)}) collective-permute-start(f32[4,4,2,8,128]{4,3,2,1,0:T(8,128)S(1)} %get-tuple-element.49), channel_id=1, source_target_pairs={{0,12},{2,14},{4,8},{6,10},{8,4},{10,6},{12,0},{14,2},{1,13},{3,15... | collective-permute-start | bytes 393224 | tf_op jit(solution)/shard_map/ppermute | solution.py:524
  26.6 10.8 %collective-permute-start.8 = (f32[4,4,2,8,128]{4,3,2,1,0:T(8,128)S(1)}, f32[4,4,2,8,128]{4,3,2,1,0:T(8,128)S(1)}, u32[]{:S(2)}, u32[]{:S(2)}) collective-permute-start(f32[4,4,2,8,128]{4,3,2,1,0:T(8,128)S(1)} %get-tuple-element.50), channel_id=1, source_target_pairs={{0,14},{2,12},{4,10},{6,8},{8,6},{10,4},{12,2},{14,0},{1,15},{3,13... | collective-permute-start | bytes 393224 | tf_op jit(solution)/shard_map/ppermute | solution.py:524
  28.3 10.7 %collective-permute-start.18 = (f32[4,4,2,8,128]{4,3,2,1,0:T(8,128)S(1)}, f32[4,4,2,8,128]{4,3,2,1,0:T(8,128)S(1)}, u32[]{:S(2)}, u32[]{:S(2)}) collective-permute-start(f32[4,4,2,8,128]{4,3,2,1,0:T(8,128)S(1)} %get-tuple-element.63), channel_id=1, source_target_pairs={{0,2},{2,0},{4,6},{6,4},{8,10},{10,8},{12,14},{14,12},{1,3},{3,1},... | collective-permute-start | bytes 393224 | tf_op jit(solution)/shard_map/ppermute | solution.py:524
  31.2 11.3 %collective-permute-start.19 = (f32[4,4,2,8,128]{4,3,2,1,0:T(8,128)S(1)}, f32[4,4,2,8,128]{4,3,2,1,0:T(8,128)S(1)}, u32[]{:S(2)}, u32[]{:S(2)}) collective-permute-start(f32[4,4,2,8,128]{4,3,2,1,0:T(8,128)S(1)} %get-tuple-element.64), channel_id=1, source_target_pairs={{0,4},{2,6},{4,0},{6,2},{8,12},{10,14},{12,8},{14,10},{1,5},{3,7},... | collective-permute-start | bytes 393224 | tf_op jit(solution)/shard_map/ppermute | solution.py:524
  31.2 14.7 %collective-permute-start.20 = (f32[4,4,2,8,128]{4,3,2,1,0:T(8,128)S(1)}, f32[4,4,2,8,128]{4,3,2,1,0:T(8,128)S(1)}, u32[]{:S(2)}, u32[]{:S(2)}) collective-permute-start(f32[4,4,2,8,128]{4,3,2,1,0:T(8,128)S(1)} %get-tuple-element.65), channel_id=1, source_target_pairs={{0,6},{2,4},{4,2},{6,0},{8,14},{10,12},{12,10},{14,8},{1,7},{3,5},... | collective-permute-start | bytes 393224 | tf_op jit(solution)/shard_map/ppermute | solution.py:524
  33.6 12.3 %collective-permute-start.21 = (f32[4,4,2,8,128]{4,3,2,1,0:T(8,128)S(1)}, f32[4,4,2,8,128]{4,3,2,1,0:T(8,128)S(1)}, u32[]{:S(2)}, u32[]{:S(2)}) collective-permute-start(f32[4,4,2,8,128]{4,3,2,1,0:T(8,128)S(1)} %get-tuple-element.66), channel_id=1, source_target_pairs={{0,8},{2,10},{4,12},{6,14},{8,0},{10,2},{12,4},{14,6},{1,9},{3,11}... | collective-permute-start | bytes 393224 | tf_op jit(solution)/shard_map/ppermute | solution.py:524
  37.4 8.5 %collective-permute-start.22 = (f32[4,4,2,8,128]{4,3,2,1,0:T(8,128)S(1)}, f32[4,4,2,8,128]{4,3,2,1,0:T(8,128)S(1)}, u32[]{:S(2)}, u32[]{:S(2)}) collective-permute-start(f32[4,4,2,8,128]{4,3,2,1,0:T(8,128)S(1)} %get-tuple-element.67), channel_id=1, source_target_pairs={{0,10},{2,8},{4,14},{6,12},{8,2},{10,0},{12,6},{14,4},{1,11},{3,9}... | collective-permute-start | bytes 393224 | tf_op jit(solution)/shard_map/ppermute | solution.py:524
  39.0 6.9 %collective-permute-start.23 = (f32[4,4,2,8,128]{4,3,2,1,0:T(8,128)S(1)}, f32[4,4,2,8,128]{4,3,2,1,0:T(8,128)S(1)}, u32[]{:S(2)}, u32[]{:S(2)}) collective-permute-start(f32[4,4,2,8,128]{4,3,2,1,0:T(8,128)S(1)} %get-tuple-element.68), channel_id=1, source_target_pairs={{0,12},{2,14},{4,8},{6,10},{8,4},{10,6},{12,0},{14,2},{1,13},{3,15... | collective-permute-start | bytes 393224 | tf_op jit(solution)/shard_map/ppermute | solution.py:524
  42.5 6.8 %collective-permute-start.24 = (f32[4,4,2,8,128]{4,3,2,1,0:T(8,128)S(1)}, f32[4,4,2,8,128]{4,3,2,1,0:T(8,128)S(1)}, u32[]{:S(2)}, u32[]{:S(2)}) collective-permute-start(f32[4,4,2,8,128]{4,3,2,1,0:T(8,128)S(1)} %get-tuple-element.69), channel_id=1, source_target_pairs={{0,14},{2,12},{4,10},{6,8},{8,6},{10,4},{12,2},{14,0},{1,15},{3,13... | collective-permute-start | bytes 393224 | tf_op jit(solution)/shard_map/ppermute | solution.py:524
  45.8 4.2 %collective-permute-start.9 = (f32[16,4096]{1,0:T(8,128)S(1)}, f32[16,4096]{1,0:T(8,128)S(1)}, u32[]{:S(2)}, u32[]{:S(2)}) collective-permute-start(f32[16,4096]{1,0:T(8,128)S(1)} %get-tuple-element.52), channel_id=1, source_target_pairs={{0,1},{1,0},{2,3},{3,2},{4,5},{5,4},{6,7},{7,6},{8,9},{9,8},{10,11... | collective-permute-start | bytes 786440 | tf_op jit(solution)/shard_map/ppermute | solution.py:592
  50.0 3.6 %collective-permute-start.25 = (f32[16,4096]{1,0:T(8,128)S(1)}, f32[16,4096]{1,0:T(8,128)S(1)}, u32[]{:S(2)}, u32[]{:S(2)}) collective-permute-start(f32[16,4096]{1,0:T(8,128)S(1)} %get-tuple-element.71), channel_id=1, source_target_pairs={{0,1},{1,0},{2,3},{3,2},{4,5},{5,4},{6,7},{7,6},{8,9},{9,8},{10,11... | collective-permute-start | bytes 786440 | tf_op jit(solution)/shard_map/ppermute | solution.py:592
  50.1 11.1 %collective-permute-start.10 = (f32[16,4096]{1,0:T(8,128)S(1)}, f32[16,4096]{1,0:T(8,128)S(1)}, u32[]{:S(2)}, u32[]{:S(2)}) collective-permute-start(f32[16,4096]{1,0:T(8,128)S(1)} %add.78.mine_ref), channel_id=1, source_target_pairs={{0,24},{2,26},{4,28},{6,30},{8,16},{10,18},{12,20},{14,22},{16,8},... | collective-permute-start | bytes 786440 | tf_op jit(solution)/shard_map/ppermute | solution.py:593
  53.6 12.7 %collective-permute-start.26 = (f32[16,4096]{1,0:T(8,128)S(1)}, f32[16,4096]{1,0:T(8,128)S(1)}, u32[]{:S(2)}, u32[]{:S(2)}) collective-permute-start(f32[16,4096]{1,0:T(8,128)S(1)} %add.79.mine_ref), channel_id=1, source_target_pairs={{0,24},{2,26},{4,28},{6,30},{8,16},{10,18},{12,20},{14,22},{16,8},... | collective-permute-start | bytes 786440 | tf_op jit(solution)/shard_map/ppermute | solution.py:593
  62.0 8.7 %collective-permute-start.11 = (f32[8,2,16,128]{3,2,1,0:T(8,128)S(1)}, f32[8,2,16,128]{3,2,1,0:T(8,128)S(1)}, u32[]{:S(2)}, u32[]{:S(2)}) collective-permute-start(f32[8,2,16,128]{3,2,1,0:T(8,128)S(1)} %bitcast.79), channel_id=1, source_target_pairs={{0,2},{2,0},{4,6},{6,4},{8,10},{10,8},{12,14},{14,12},{1,3},{3,1},... | collective-permute-start | bytes 393224 | tf_op jit(solution)/shard_map/ppermute | solution.py:524
  63.2 18.5 %collective-permute-start.12 = (f32[8,2,16,128]{3,2,1,0:T(8,128)S(1)}, f32[8,2,16,128]{3,2,1,0:T(8,128)S(1)}, u32[]{:S(2)}, u32[]{:S(2)}) collective-permute-start(f32[8,2,16,128]{3,2,1,0:T(8,128)S(1)} %bitcast.78), channel_id=1, source_target_pairs={{0,4},{2,6},{4,0},{6,2},{8,12},{10,14},{12,8},{14,10},{1,5},{3,7},... | collective-permute-start | bytes 393224 | tf_op jit(solution)/shard_map/ppermute | solution.py:524
  67.2 14.9 %collective-permute-start.27 = (f32[8,2,16,128]{3,2,1,0:T(8,128)S(1)}, f32[8,2,16,128]{3,2,1,0:T(8,128)S(1)}, u32[]{:S(2)}, u32[]{:S(2)}) collective-permute-start(f32[8,2,16,128]{3,2,1,0:T(8,128)S(1)} %bitcast.81), channel_id=1, source_target_pairs={{0,2},{2,0},{4,6},{6,4},{8,10},{10,8},{12,14},{14,12},{1,3},{3,1},... | collective-permute-start | bytes 393224 | tf_op jit(solution)/shard_map/ppermute | solution.py:524
  68.3 15.2 %collective-permute-start.28 = (f32[8,2,16,128]{3,2,1,0:T(8,128)S(1)}, f32[8,2,16,128]{3,2,1,0:T(8,128)S(1)}, u32[]{:S(2)}, u32[]{:S(2)}) collective-permute-start(f32[8,2,16,128]{3,2,1,0:T(8,128)S(1)} %bitcast.80), channel_id=1, source_target_pairs={{0,4},{2,6},{4,0},{6,2},{8,12},{10,14},{12,8},{14,10},{1,5},{3,7},... | collective-permute-start | bytes 393224 | tf_op jit(solution)/shard_map/ppermute | solution.py:524
  69.0 17.4 %collective-permute-start.29 = (f32[8,2,16,128]{3,2,1,0:T(8,128)S(1)}, f32[8,2,16,128]{3,2,1,0:T(8,128)S(1)}, u32[]{:S(2)}, u32[]{:S(2)}) collective-permute-start(f32[8,2,16,128]{3,2,1,0:T(8,128)S(1)} %bitcast.77), channel_id=1, source_target_pairs={{0,6},{2,4},{4,2},{6,0},{8,14},{10,12},{12,10},{14,8},{1,7},{3,5},... | collective-permute-start | bytes 393224 | tf_op jit(solution)/shard_map/ppermute | solution.py:524
  70.7 19.0 %collective-permute-start.30 = (f32[8,2,16,128]{3,2,1,0:T(8,128)S(1)}, f32[8,2,16,128]{3,2,1,0:T(8,128)S(1)}, u32[]{:S(2)}, u32[]{:S(2)}) collective-permute-start(f32[8,2,16,128]{3,2,1,0:T(8,128)S(1)} %bitcast.76), channel_id=1, source_target_pairs={{0,8},{2,10},{4,12},{6,14},{8,0},{10,2},{12,4},{14,6},{1,9},{3,11}... | collective-permute-start | bytes 393224 | tf_op jit(solution)/shard_map/ppermute | solution.py:524
  81.7 8.1 %collective-permute-start.31 = (f32[8,2,16,128]{3,2,1,0:T(8,128)S(1)}, f32[8,2,16,128]{3,2,1,0:T(8,128)S(1)}, u32[]{:S(2)}, u32[]{:S(2)}) collective-permute-start(f32[8,2,16,128]{3,2,1,0:T(8,128)S(1)} %bitcast.75), channel_id=1, source_target_pairs={{0,10},{2,8},{4,14},{6,12},{8,2},{10,0},{12,6},{14,4},{1,11},{3,9}... | collective-permute-start | bytes 393224 | tf_op jit(solution)/shard_map/ppermute | solution.py:524
  82.1 9.8 %collective-permute-start.32 = (f32[8,2,16,128]{3,2,1,0:T(8,128)S(1)}, f32[8,2,16,128]{3,2,1,0:T(8,128)S(1)}, u32[]{:S(2)}, u32[]{:S(2)}) collective-permute-start(f32[8,2,16,128]{3,2,1,0:T(8,128)S(1)} %bitcast.74), channel_id=1, source_target_pairs={{0,12},{2,14},{4,8},{6,10},{8,4},{10,6},{12,0},{14,2},{1,13},{3,15... | collective-permute-start | bytes 393224 | tf_op jit(solution)/shard_map/ppermute | solution.py:524
  83.5 11.9 %collective-permute-start.33 = (f32[8,2,16,128]{3,2,1,0:T(8,128)S(1)}, f32[8,2,16,128]{3,2,1,0:T(8,128)S(1)}, u32[]{:S(2)}, u32[]{:S(2)}) collective-permute-start(f32[8,2,16,128]{3,2,1,0:T(8,128)S(1)} %bitcast.73), channel_id=1, source_target_pairs={{0,14},{2,12},{4,10},{6,8},{8,6},{10,4},{12,2},{14,0},{1,15},{3,13... | collective-permute-start | bytes 393224 | tf_op jit(solution)/shard_map/ppermute | solution.py:524
  86.4 14.4 %collective-permute-start.13 = (f32[8,2,16,128]{3,2,1,0:T(8,128)S(1)}, f32[8,2,16,128]{3,2,1,0:T(8,128)S(1)}, u32[]{:S(2)}, u32[]{:S(2)}) collective-permute-start(f32[8,2,16,128]{3,2,1,0:T(8,128)S(1)} %bitcast.72), channel_id=1, source_target_pairs={{0,6},{2,4},{4,2},{6,0},{8,14},{10,12},{12,10},{14,8},{1,7},{3,5},... | collective-permute-start | bytes 393224 | tf_op jit(solution)/shard_map/ppermute | solution.py:524
  89.8 11.0 %collective-permute-start.14 = (f32[8,2,16,128]{3,2,1,0:T(8,128)S(1)}, f32[8,2,16,128]{3,2,1,0:T(8,128)S(1)}, u32[]{:S(2)}, u32[]{:S(2)}) collective-permute-start(f32[8,2,16,128]{3,2,1,0:T(8,128)S(1)} %bitcast.71), channel_id=1, source_target_pairs={{0,8},{2,10},{4,12},{6,14},{8,0},{10,2},{12,4},{14,6},{1,9},{3,11}... | collective-permute-start | bytes 393224 | tf_op jit(solution)/shard_map/ppermute | solution.py:524
  89.8 10.9 %collective-permute-start.15 = (f32[8,2,16,128]{3,2,1,0:T(8,128)S(1)}, f32[8,2,16,128]{3,2,1,0:T(8,128)S(1)}, u32[]{:S(2)}, u32[]{:S(2)}) collective-permute-start(f32[8,2,16,128]{3,2,1,0:T(8,128)S(1)} %bitcast.70), channel_id=1, source_target_pairs={{0,10},{2,8},{4,14},{6,12},{8,2},{10,0},{12,6},{14,4},{1,11},{3,9}... | collective-permute-start | bytes 393224 | tf_op jit(solution)/shard_map/ppermute | solution.py:524
  91.9 10.0 %collective-permute-start.16 = (f32[8,2,16,128]{3,2,1,0:T(8,128)S(1)}, f32[8,2,16,128]{3,2,1,0:T(8,128)S(1)}, u32[]{:S(2)}, u32[]{:S(2)}) collective-permute-start(f32[8,2,16,128]{3,2,1,0:T(8,128)S(1)} %bitcast.69), channel_id=1, source_target_pairs={{0,12},{2,14},{4,8},{6,10},{8,4},{10,6},{12,0},{14,2},{1,13},{3,15... | collective-permute-start | bytes 393224 | tf_op jit(solution)/shard_map/ppermute | solution.py:524
  95.4 8.7 %collective-permute-start.17 = (f32[8,2,16,128]{3,2,1,0:T(8,128)S(1)}, f32[8,2,16,128]{3,2,1,0:T(8,128)S(1)}, u32[]{:S(2)}, u32[]{:S(2)}) collective-permute-start(f32[8,2,16,128]{3,2,1,0:T(8,128)S(1)} %bitcast.68), channel_id=1, source_target_pairs={{0,14},{2,12},{4,10},{6,8},{8,6},{10,4},{12,2},{14,0},{1,15},{3,13... | collective-permute-start | bytes 393224 | tf_op jit(solution)/shard_map/ppermute | solution.py:524
  (10 other events, 70.7 us)
